TPU v7x, 512 devices: a whole 4x4x16 slice. The times are simulated.
512 devices in a mesh: seq: 128 (over x, z, core), head: 4 (over y).
Axes of the slice: x: 4, y: 4, z: 16, core: 2. Of those that a mesh axis runs over, the one named last changes fastest.
Arguments:
- tokens: bfloat16 [128, 128, 2048], P('seq'), may hold values from -6 to 6
- attn_gain: bfloat16 [2048], replicated, may hold values from 0.099609375 to 1.8984375
- q_gain: bfloat16 [64], replicated, may hold values from 0.099609375 to 1.8984375
- k_gain: bfloat16 [64], replicated, may hold values from 0.099609375 to 1.8984375
- ffn_gain: bfloat16 [2048], replicated, may hold values from 0.099609375 to 1.8984375
- w_query: bfloat16 [2048, 1280], P('seq', 'head'), may hold values from -0.125 to 0.125
- w_keyval: bfloat16 [2048, 640], P('seq'), may hold values from -0.125 to 0.125
- w_out: bfloat16 [1280, 2048], P('head', 'seq'), may hold values from -0.15625 to 0.15625
- prior_cache: bfloat16 [128, 512, 640], P(None, 'seq')
- prior_len: int32 [128], replicated, may hold values from 0 to 512, as said below
- stretch_len: int32 [128], replicated, may hold values from 1 to 128, as said below
Outputs:
- hidden: bfloat16 [128, 128, 2048], P('seq', 'head')
- ffn_input: bfloat16 [128, 128, 2048], P('seq', 'head')
- new_cache: bfloat16 [128, 128, 640], P('seq', 'head')
- decode_cache: bfloat16 [128, 512, 640], P('seq', 'head')
Inputs may be any that keep to these rules, and one draw needn't show every extreme that they name: `prior_len`: some request has all 512 slots in use. `stretch_len`: some request fills its stretch.
All inputs are finite; a program needn't handle non-finite values.
Results may differ from a plain program's by a relative error of at most 0.011.
The roundings to bfloat16 on the way count: a program that leaves them out, or rounds other values in their place, can miss the bound.
Values may be sent and summed in bfloat16 or wider, within the bound.
A program may use at most 64 MiB of HBM per device.

v0:
```python
import math

import jax
import jax.numpy as jnp
from jax import lax
from jax.sharding import PartitionSpec as P

HD = 64
QH = 20
KVH = 5


epsilon = 1e-06


def rms_norm(values, gain):
    return values * lax.rsqrt(jnp.mean(values * values, axis=-1, keepdims=True) + epsilon) * gain


def rotary(values, positions):
    middle = values.shape[-1] // 2
    inverse = jnp.exp(
        jnp.arange(middle, dtype=jnp.float32) * (-2.0 * math.log(10000.0) / values.shape[-1])
    )
    angles = positions.astype(jnp.float32)[:, None] * inverse[None, :]
    cosine = jnp.concatenate([jnp.cos(angles), jnp.cos(angles)], axis=-1)[:, None, :]
    sine = jnp.concatenate([jnp.sin(angles), jnp.sin(angles)], axis=-1)[:, None, :]
    turned = jnp.concatenate([-values[..., middle:], values[..., :middle]], axis=-1)
    return values * cosine + turned * sine


def attend_dense(
    query, prior_keys, prior_values, fresh_keys, fresh_values, prior_count, score_scale
):
    length = fresh_keys.shape[0]
    stored = prior_keys.shape[0]
    all_keys = jnp.concatenate([prior_keys, fresh_keys], axis=0)
    all_values = jnp.concatenate([prior_values, fresh_values], axis=0)
    scores = (
        jnp.einsum("qhd,khd->hqk", query, all_keys, preferred_element_type=jnp.float32)
        * score_scale
    )
    offsets = jnp.arange(length, dtype=jnp.int32)
    earlier = jnp.arange(stored, dtype=jnp.int32)[None, :] < prior_count
    allowed = jnp.concatenate(
        [jnp.broadcast_to(earlier, (length, stored)), offsets[None, :] <= offsets[:, None]], axis=1
    )
    scores = jnp.where(allowed[None], scores, -jnp.inf)
    top = jnp.max(scores, axis=-1, keepdims=True)
    weights = jnp.exp(scores - top)
    total = jnp.sum(weights, axis=-1)
    mixed = jnp.einsum(
        "hqk,khd->qhd", weights.astype(jnp.bfloat16), all_values, preferred_element_type=jnp.float32
    )
    return mixed / total.T[:, :, None]


def shards(
    tokens,
    attn_gain,
    q_gain,
    k_gain,
    ffn_gain,
    w_query,
    w_keyval,
    w_out,
    prior_cache,
    prior_len,
    stretch_len,
):
    seq_index = lax.axis_index("seq")
    head_index = lax.axis_index("head")
    head_count = lax.axis_size("head")
    local_requests, length, width = tokens.shape
    token_count = local_requests * length
    width_kv = KVH * HD
    local_heads = QH // head_count
    score_scale = 1.0 / math.sqrt(HD)
    flat = tokens.reshape(token_count, width)
    normed = rms_norm(flat.astype(jnp.float32), attn_gain.astype(jnp.float32)).astype(jnp.bfloat16)
    first = jnp.dot(
        normed,
        lax.all_gather(w_query, "seq", axis=0, tiled=True),
        preferred_element_type=jnp.float32,
    )
    second = jnp.dot(
        normed,
        lax.all_gather(w_keyval, "seq", axis=0, tiled=True),
        preferred_element_type=jnp.float32,
    )
    query = first
    prior_counts = lax.dynamic_slice_in_dim(prior_len, seq_index * local_requests, local_requests)
    stretch_counts = lax.dynamic_slice_in_dim(
        stretch_len, seq_index * local_requests, local_requests
    )
    offsets = jnp.arange(length, dtype=jnp.int32)
    positions = (prior_counts[:, None] + offsets[None, :]).reshape(token_count)
    query = rotary(
        rms_norm(query.reshape(token_count, local_heads, HD), q_gain.astype(jnp.float32)), positions
    ).astype(jnp.bfloat16)
    fresh_keys = rotary(
        rms_norm(second[:, :width_kv].reshape(token_count, KVH, HD), k_gain.astype(jnp.float32)),
        positions,
    ).astype(jnp.bfloat16)
    fresh_values = second[:, width_kv:].reshape(token_count, KVH, HD).astype(jnp.bfloat16)
    gathered_cache = lax.all_to_all(prior_cache, "seq", split_axis=0, concat_axis=1, tiled=True)
    stored = gathered_cache.shape[1]
    block_slots = stored // head_count
    decode_cache = lax.dynamic_slice_in_dim(
        gathered_cache, head_index * block_slots, block_slots, 1
    )
    group = (head_index * local_heads + jnp.arange(local_heads, dtype=jnp.int32)) // (QH // KVH)
    prior_keys = jnp.take(
        gathered_cache[:, :, :width_kv].reshape(local_requests, stored, KVH, HD), group, axis=2
    )
    prior_values = jnp.take(
        gathered_cache[:, :, width_kv:].reshape(local_requests, stored, KVH, HD), group, axis=2
    )
    stretch_keys = jnp.take(fresh_keys.reshape(local_requests, length, KVH, HD), group, axis=2)
    stretch_values = jnp.take(fresh_values.reshape(local_requests, length, KVH, HD), group, axis=2)
    query_blocks = query.reshape(local_requests, length, local_heads, HD)
    mixed = attend_dense(
        query_blocks[0],
        prior_keys[0],
        prior_values[0],
        stretch_keys[0],
        stretch_values[0],
        prior_counts[0],
        score_scale,
    )
    results = mixed.astype(jnp.bfloat16).reshape(length, local_heads * HD)
    terms = jnp.dot(
        results,
        lax.all_gather(w_out, "seq", axis=1, tiled=True),
        preferred_element_type=jnp.float32,
    )
    share_rows = length // head_count
    summed = lax.psum_scatter(
        terms.reshape(local_requests, length, width).astype(jnp.bfloat16),
        "head",
        scatter_dimension=1,
        tiled=True,
    ).astype(jnp.float32)
    own_tokens = lax.dynamic_slice_in_dim(tokens, head_index * share_rows, share_rows, 1).astype(
        jnp.float32
    )
    residual = own_tokens + summed
    row_offsets = head_index * share_rows + jnp.arange(share_rows, dtype=jnp.int32)
    valid = row_offsets[None, :] < stretch_counts[:, None]
    hidden = jnp.where(valid[:, :, None], residual, 0.0).astype(jnp.bfloat16)
    ffn_input = jnp.where(
        valid[:, :, None], rms_norm(residual, ffn_gain.astype(jnp.float32)), 0.0
    ).astype(jnp.bfloat16)
    fresh = jnp.concatenate(
        [
            fresh_keys.reshape(local_requests, length, width_kv),
            fresh_values.reshape(local_requests, length, width_kv),
        ],
        axis=2,
    )
    fresh = lax.dynamic_slice_in_dim(fresh, head_index * share_rows, share_rows, 1)
    fresh = jnp.where(valid[:, :, None], fresh, jnp.zeros_like(fresh))
    return (hidden, ffn_input, fresh, decode_cache)


def solution(mesh):
    placed = (
        P("seq", None, None),
        P(),
        P(),
        P(),
        P(),
        P("seq", "head"),
        P("seq", None),
        P("head", "seq"),
        P(None, "seq", None),
        P(),
        P(),
    )
    return jax.shard_map(
        shards,
        mesh=mesh,
        in_specs=placed,
        out_specs=(
            P("seq", "head", None),
            P("seq", "head", None),
            P("seq", "head", None),
            P("seq", "head", None),
        ),
        check_vma=False,
    )
```

profile of v0, /device:TPU:1, one launch (start us, length us, event | category | flops | bytes accessed | tf_op | source)
XLA Modules:
  0.0 472.9 jit_solution(8410260316562523940)
XLA Ops:
  7.2 0.7 all-gather.6.cloned.1.call-update
  8.0 0.7 all-gather.4.cloned.1.call-update
  8.7 20.4 %all-to-all-start = ((bf16[128,4,640]{2,1,0:T(4,128)(2,1)}), bf16[128,4,640]{2,1,0:T(4,128)(2,1)S(1)}, u32[]{:S(2)}, u32[]{:S(2)}) async-start(bf16[128,4,640]{2,1,0:T(4,128)(2,1)} %param.23), calls=%async_computation | async-start | bytes 1310720 | tf_op jit(solution)/shard_map/all_to_all | solution.py:106
  29.1 0.7 all-gather.8.cloned.1.call-update
  29.8 0.7 convert_element_type.100
  30.5 0.7 convert_element_type.110
  31.2 0.7 convert_element_type.107
  31.9 1.2 dynamic_slice.17
  33.1 0.6 iota_compare_fusion.1
  33.8 0.7 add_convert_fusion
  34.9 32.9 %all-to-all-done = bf16[128,4,640]{2,1,0:T(4,128)(2,1)S(1)} async-done(((bf16[128,4,640]{2,1,0:T(4,128)(2,1)}), bf16[128,4,640]{2,1,0:T(4,128)(2,1)S(1)}, u32[]{:S(2)}, u32[]{:S(2)}) %all-to-all-start) | async-done | bytes 655392 | tf_op jit(solution)/shard_map/all_to_all | solution.py:106
  68.2 89.4 %all-gather.6.cloned.1.call-done = bf16[2048,320]{1,0:T(8,128)(2,1)} async-done(((bf16[16,320]{1,0:T(8,128)(2,1)}), bf16[2048,320]{1,0:T(8,128)(2,1)}) %all-gather.6.cloned.1.call-update) | async-done | bytes 1310736 | tf_op jit(solution)/shard_map/all_gather | solution.py:83
  157.6 1.7 copy.41
  159.3 0.6 multiply_reduce_fusion.2
  160.3 0.6 gather_fusion
  160.9 0.6 gather_fusion.2
  161.6 136.5 %all-gather.4.cloned.1.call-done = bf16[2048,640]{1,0:T(8,128)(2,1)} async-done(((bf16[16,640]{1,0:T(8,128)(2,1)}), bf16[2048,640]{1,0:T(8,128)(2,1)}) %all-gather.4.cloned.1.call-update) | async-done | bytes 2621456 | tf_op jit(solution)/shard_map/all_gather | solution.py:88
  298.1 2.9 fusion.17
  301.1 0.6 gather_fusion.1
  301.9 0.6 gather_fusion.3
  302.6 0.5 fusion.49
  303.1 0.5 fusion.1
  303.6 0.5 fusion.6
  304.1 133.6 %all-gather.8.cloned.1.call-done = bf16[320,2048]{0,1:T(8,128)(2,1)} async-done(((bf16[320,16]{0,1:T(8,128)(2,1)}), bf16[320,2048]{0,1:T(8,128)(2,1)}) %all-gather.8.cloned.1.call-update) | async-done | bytes 1310736 | tf_op jit(solution)/shard_map/all_gather | solution.py:134
  437.7 2.8 fusion
  440.6 0.6 dynamic_slice.15
  441.3 0.7 add_compare_fusion
  441.9 0.7 constant_dynamic-slice_fusion
  442.9 0.7 copy.44
  443.6 20.0 %reduce-scatter.2.cloned.1.call-done = bf16[1,32,2048]{2,1,0:T(8,128)(2,1)} async-done(((bf16[1,128,2048]{2,1,0:T(8,128)(2,1)}), bf16[1,32,2048]{2,1,0:T(8,128)(2,1)}) %reduce-scatter.2.cloned.1.call-update) | async-done | bytes 131088 | tf_op jit(solution)/shard_map/reduce_scatter | solution.py:138
  463.6 1.1 multiply_reduce_fusion
  464.7 1.7 select_convert_fusion
  (48 shorter events, 2.2 us)
Async XLA Ops:
  7.2 27.5 %copy-start = (bf16[1,128,2048]{2,1,0:T(8,128)(2,1)S(1)}, bf16[1,128,2048]{2,1,0:T(8,128)(2,1)}, u32[]{:S(2)}) copy-start(bf16[1,128,2048]{2,1,0:T(8,128)(2,1)} %param.15) | copy-start | bytes 1572868
  7.2 150.4 %all-gather.6.cloned.1.call-start = ((), (), s32[]{:S(2)}) async-start(), calls=%async_computation.3 | async-start | bytes 1585152 | tf_op jit(solution)/shard_map/all_gather | solution.py:83
  7.9 290.2 %all-gather.4.cloned.1.call-start = ((), (), s32[]{:S(2)}) async-start(), calls=%async_computation.2 | async-start | bytes 2641920 | tf_op jit(solution)/shard_map/all_gather | solution.py:88
  8.7 59.2 %all-to-all-start = ((bf16[128,4,640]{2,1,0:T(4,128)(2,1)}), bf16[128,4,640]{2,1,0:T(4,128)(2,1)S(1)}, u32[]{:S(2)}, u32[]{:S(2)}) async-start(bf16[128,4,640]{2,1,0:T(4,128)(2,1)} %param.23), calls=%async_computation | async-start | bytes 1310720 | tf_op jit(solution)/shard_map/all_to_all | solution.py:106
  29.1 408.6 %all-gather.8.cloned.1.call-start = ((), (), s32[]{:S(2)}) async-start(), calls=%async_computation.4 | async-start | bytes 1585152 | tf_op jit(solution)/shard_map/all_gather | solution.py:134
  29.8 433.8 %reduce-scatter.2.cloned.1.call-start = ((), (), s32[]{:S(2)}) async-start(), calls=%async_computation.5 | async-start | bytes 655360 | tf_op jit(solution)/shard_map/reduce_scatter | solution.py:138
  304.1 136.5 %copy-start.1 = (bf16[2048]{0:T(1024)(128)(2,1)S(1)}, bf16[2048]{0:T(1024)(128)(2,1)}, u32[]{:S(2)}) copy-start(bf16[2048]{0:T(1024)(128)(2,1)} %param.19) | copy-start | bytes 12292
  304.1 136.5 %copy-start.3 = (s32[128]{0:T(128)S(1)}, s32[128]{0:T(128)}, u32[]{:S(2)}) copy-start(s32[128]{0:T(128)} %param.25) | copy-start | bytes 1540
  304.1 137.1 %copy-start.2 = (bf16[64]{0:T(256)(128)(2,1)S(1)}, bf16[64]{0:T(256)(128)(2,1)}, u32[]{:S(2)}) copy-start(bf16[64]{0:T(256)(128)(2,1)} %param.18) | copy-start | bytes 388
Sparse Core Ops, SparseCore 0:
  11.0 146.4 all-gather.5
  160.6 137.4 all-gather.3
  301.2 136.4 all-gather.7
  440.7 22.8 reduce-scatter.1
where the time goes:
time: 475 us; the launch traced here: 473 us
  waiting for transfers between devices  414 us (87%)
  starting transfers between devices  20.5 us (4%)
  between operations  14.1 us (3%)
  other arithmetic  8.47 us (2%)
  local copies, waits for them, and re-layouts  8.03 us (2%)
  matrix products  7.37 us (2%)
    all_gather x1, waiting for transfers between devices, shards(): lax.all_gather(w_keyval, 'seq', axis=0, tiled=True)  136 us
    all_gather x1, waiting for transfers between devices, shards(): lax.all_gather(w_out, 'seq', axis=1, tiled=True)  134 us
    all_gather x1, waiting for transfers between devices, shards(): lax.all_gather(w_query, 'seq', axis=0, tiled=True)  89.4 us
    all_to_all x1, waiting for transfers between devices, shards(): lax.all_to_all(prior_cache, 'seq', split_axis=0, concat_axis=1, tiled=True)  32.9 us
    all_to_all x1, starting transfers between devices, shards(): lax.all_to_all(prior_cache, 'seq', split_axis=0, concat_axis=1, tiled=True)  20.4 us
    reduce_scatter x1, waiting for transfers between devices, shards(): lax.psum_scatter(terms.reshape(local_requests, length, width).astype(jnp....  20 us
  transfers between devices with their start and end apart: 5, of which 5 were waited for; matrix products, arithmetic and copies ran while one was open for 4% of the time, Pallas kernels for 0%

commit v1 on v0

v1 whole, which is shorter than its diff:
```python
import math

import jax
import jax.numpy as jnp
from jax import lax
from jax.experimental import pallas as pl
from jax.experimental.pallas import tpu as pltpu
from jax.sharding import PartitionSpec as P

HD = 64
QH = 20
KVH = 5
NX, NZ, NY = 4, 16, 4
PLANE = NZ * 2
WIDE = 896
MESH = pl.DeviceIdType.MESH

epsilon = 1e-06


def rms_norm(values, gain):
    return values * lax.rsqrt(jnp.mean(values * values, axis=-1, keepdims=True) + epsilon) * gain


def rotary(values, positions):
    middle = values.shape[-1] // 2
    inverse = jnp.exp(
        jnp.arange(middle, dtype=jnp.float32) * (-2.0 * math.log(10000.0) / values.shape[-1])
    )
    angles = positions.astype(jnp.float32)[:, None] * inverse[None, :]
    cosine = jnp.concatenate([jnp.cos(angles), jnp.cos(angles)], axis=-1)[:, None, :]
    sine = jnp.concatenate([jnp.sin(angles), jnp.sin(angles)], axis=-1)[:, None, :]
    turned = jnp.concatenate([-values[..., middle:], values[..., :middle]], axis=-1)
    return values * cosine + turned * sine


def tile_of(head, j):
    first = jnp.where(head >= 2, 1, 0)
    second = jnp.where(head == 0, 2, jnp.where(head == 1, 1, jnp.where(head == 2, 3, 2)))
    third = jnp.where(head >= 2, 4, 3)
    return (first, second, third)[j]


def gather_kernel(
    pack_ref, cache_ref, w_ref, d_ref, e_ref, x_buf, w_send, w_recv, x_send, x_recv, d_send, d_recv, e_send, e_recv
):
    s = lax.axis_index("seq")
    h = lax.axis_index("head")
    x = s // PLANE
    low = lax.rem(s, PLANE)
    z = low // 2
    c = lax.rem(low, 2)

    def sid(xx, zz, cc):
        return xx * PLANE + zz * 2 + cc

    def wrapx(v):
        return lax.rem(v + NX, NX)

    def wrapz(v):
        return lax.rem(v + NZ, NZ)

    barrier = pltpu.get_barrier_semaphore()

    def greet(k, carry):
        pl.semaphore_signal(
            barrier, inc=1, device_id={"seq": x * PLANE + lax.rem(low + k, PLANE)}, device_id_type=MESH
        )
        return carry

    lax.fori_loop(1, PLANE, greet, 0)
    for k in range(1, NX):
        pl.semaphore_signal(
            barrier, inc=1, device_id={"seq": sid(wrapx(x + k), z, c)}, device_id_type=MESH
        )
    for k in range(1, NY):
        pl.semaphore_signal(
            barrier, inc=1, device_id={"head": lax.rem(h + k, NY)}, device_id_type=MESH
        )
    pl.semaphore_wait(barrier, PLANE - 1 + NX - 1 + NY - 1)

    mine = cache_ref.at[pl.ds(pl.multiple_of(x * PLANE, PLANE), PLANE)]

    @pl.when(x == h)
    def _():
        for k in range(1, NX):
            xx = wrapx(x + k)
            pltpu.make_async_remote_copy(
                src_ref=cache_ref.at[pl.ds(pl.multiple_of(xx * PLANE, PLANE), PLANE)],
                dst_ref=x_buf,
                send_sem=x_send.at[k - 1],
                recv_sem=x_recv,
                device_id={"seq": sid(xx, z, c)},
                device_id_type=MESH,
            ).start()
        pltpu.make_async_copy(mine, x_buf, x_recv).start()

    ahead = jnp.where(c == 0, 1, -1)
    partner = {"seq": sid(x, z, 1 - c)}

    def rows(b):
        return w_ref.at[pl.ds(pl.multiple_of(b * 16, 16), 16)]

    def push(b, target, src=None):
        pltpu.make_async_remote_copy(
            src_ref=rows(b) if src is None else src,
            dst_ref=rows(b),
            send_sem=w_send,
            recv_sem=w_recv.at[b],
            device_id=target,
            device_id_type=MESH,
        ).start()

    def arrive(b):
        pltpu.make_async_copy(rows(b), rows(b), w_recv.at[b]).wait()

    along = {"seq": sid(wrapx(x + ahead), z, c)}
    against = {"seq": sid(wrapx(x - ahead), z, c)}
    up = {"seq": sid(x, wrapz(z + 1), c)}
    down = {"seq": sid(x, wrapz(z - 1), c)}

    pltpu.make_async_copy(pack_ref, rows(s), w_recv.at[s]).start()
    push(s, up, pack_ref)
    push(s, down, pack_ref)
    push(s, along, pack_ref)
    push(s, against, pack_ref)
    push(s, partner, pack_ref)

    def spread(b):
        push(b, along)
        push(b, against)
        push(b, partner)

    def relay(zb):
        b = sid(wrapx(x - ahead), zb, c)
        arrive(b)
        push(b, along)
        push(b, partner)
        b = sid(wrapx(x + ahead), zb, c)
        arrive(b)
        push(b, partner)

    def last(zb):
        b = sid(wrapx(x + 2), zb, c)
        arrive(b)
        push(b, partner)

    HALF = NZ // 2
    for t in range(1, HALF + 1):
        b = sid(x, wrapz(z - t), c)
        arrive(b)
        if t < HALF:
            push(b, up)
        spread(b)
        if t < HALF:
            b = sid(x, wrapz(z + t), c)
            arrive(b)
            if t < HALF - 1:
                push(b, down)
            spread(b)
        if t == 2:
            pltpu.make_async_copy(x_buf, x_buf, x_recv).wait()

            def hand(k, carry):
                to = lax.rem(low + k, PLANE)
                pltpu.make_async_remote_copy(
                    src_ref=x_buf.at[to],
                    dst_ref=d_ref.at[low],
                    send_sem=d_send,
                    recv_sem=d_recv,
                    device_id={"seq": x * PLANE + to},
                    device_id_type=MESH,
                ).start()
                return carry

            lax.fori_loop(1, PLANE, hand, 0)
            pltpu.make_async_copy(x_buf.at[low], d_ref.at[low], d_recv).start()
        u = t - 2
        if u == 0:
            relay(z)
        if 0 < u < HALF:
            relay(wrapz(z - u))
            relay(wrapz(z + u))
        u = t - 4
        if u == 0:
            last(z)
        if 0 < u < HALF:
            last(wrapz(z - u))
            last(wrapz(z + u))
    pltpu.make_async_copy(d_ref, d_ref, d_recv).wait()
    for k in range(1, NY):
        to = lax.rem(h + k, NY)
        for j in range(3):
            pltpu.make_async_remote_copy(
                src_ref=d_ref.at[:, :, pl.ds(pl.multiple_of(tile_of(to, j) * 128, 128), 128)],
                dst_ref=e_ref.at[h, j],
                send_sem=e_send,
                recv_sem=e_recv,
                device_id={"head": to},
                device_id_type=MESH,
            ).start()
    for j in range(3):
        pltpu.make_async_copy(
            d_ref.at[:, :, pl.ds(pl.multiple_of(tile_of(h, j) * 128, 128), 128)], e_ref.at[h, j], e_recv
        ).start()
    relay(wrapz(z - HALF + 1))
    relay(wrapz(z + HALF - 1))
    relay(wrapz(z + HALF))
    for u in range(HALF - 3, HALF):
        last(wrapz(z - u))
        last(wrapz(z + u))
    last(wrapz(z + HALF))

    arrive(s)
    other = s + 1 - 2 * c

    def shared(k, carry):
        b = (s // 2 * 2 + 2 * k + 1 - c) % (NX * PLANE)
        arrive(b)
        return carry

    lax.fori_loop(0, NX * NZ, shared, 0)
    pltpu.make_async_copy(e_ref, e_ref, e_recv).wait()
    for k in range(NX - 1):

        @pl.when(x == h)
        def _(k=k):
            pltpu.make_async_copy(mine, mine, x_send.at[k]).wait()

    pltpu.make_async_copy(d_ref.at[pl.ds(0, PLANE - 1)], d_ref.at[pl.ds(0, PLANE - 1)], d_send).wait()
    pltpu.make_async_copy(e_ref.at[pl.ds(0, NY - 1)], e_ref.at[pl.ds(0, NY - 1)], e_send).wait()
    sent = 2 * NX * NZ - 1
    pltpu.make_async_copy(w_ref.at[pl.ds(0, sent * 16)], w_ref.at[pl.ds(0, sent * 16)], w_send).wait()


def gather(pack, cache):
    vmem = pl.BlockSpec(memory_space=pltpu.VMEM)
    return pl.pallas_call(
        gather_kernel,
        out_shape=(
            jax.ShapeDtypeStruct((2048, WIDE), jnp.bfloat16),
            jax.ShapeDtypeStruct((PLANE, 4, 640), jnp.bfloat16),
            jax.ShapeDtypeStruct((NY, 3, PLANE, 4, 128), jnp.bfloat16),
        ),
        in_specs=[vmem, pl.BlockSpec(memory_space=pl.ANY)],
        out_specs=(vmem, vmem, vmem),
        scratch_shapes=[
            pltpu.VMEM((PLANE, 4, 640), jnp.bfloat16),
            pltpu.SemaphoreType.DMA,
            pltpu.SemaphoreType.DMA((NX * PLANE,)),
            pltpu.SemaphoreType.DMA((NX - 1,)),
            pltpu.SemaphoreType.DMA,
            pltpu.SemaphoreType.DMA,
            pltpu.SemaphoreType.DMA,
            pltpu.SemaphoreType.DMA,
            pltpu.SemaphoreType.DMA,
        ],
        compiler_params=pltpu.CompilerParams(collective_id=0, has_side_effects=True),
        name="gather",
    )(pack, cache)


def swap_kernel(terms_ref, kv_ref, t_ref, k_ref, t_send, t_recv, k_send, k_recv):
    h = lax.axis_index("head")
    barrier = pltpu.get_barrier_semaphore()
    for k in range(1, NY):
        pl.semaphore_signal(
            barrier, inc=1, device_id={"head": lax.rem(h + k, NY)}, device_id_type=MESH
        )
    pl.semaphore_wait(barrier, NY - 1)
    for k in (2, 1, 3):
        to = lax.rem(h + k, NY)
        for src, dst, ss, rs in ((terms_ref, t_ref, t_send, t_recv), (kv_ref, k_ref, k_send, k_recv)):
            pltpu.make_async_remote_copy(
                src_ref=src.at[to],
                dst_ref=dst.at[h],
                send_sem=ss,
                recv_sem=rs,
                device_id={"head": to},
                device_id_type=MESH,
            ).start()
    pltpu.make_async_copy(terms_ref.at[h], t_ref.at[h], t_recv).start()
    pltpu.make_async_copy(kv_ref.at[h], k_ref.at[h], k_recv).start()
    for ref, ss, rs in ((t_ref, t_send, t_recv), (k_ref, k_send, k_recv)):
        pltpu.make_async_copy(ref, ref, rs).wait()
        part = ref.at[pl.ds(0, NY - 1)]
        pltpu.make_async_copy(part, part, ss).wait()


def swap(terms, kv):
    vmem = pl.BlockSpec(memory_space=pltpu.VMEM)
    return pl.pallas_call(
        swap_kernel,
        out_shape=(
            jax.ShapeDtypeStruct(terms.shape, terms.dtype),
            jax.ShapeDtypeStruct(kv.shape, kv.dtype),
        ),
        in_specs=[vmem, vmem],
        out_specs=(vmem, vmem),
        scratch_shapes=[pltpu.SemaphoreType.DMA] * 4,
        compiler_params=pltpu.CompilerParams(collective_id=1, has_side_effects=True),
        name="swap",
    )(terms, kv)


def half_swap(a, b):
    return jnp.concatenate([a[:, 64:], b[:, :64]], axis=1)


def shards(tokens, attn_gain, q_gain, k_gain, ffn_gain, w_query, w_keyval, w_out, prior_cache, prior_len, stretch_len):
    seq_index = lax.axis_index("seq")
    h = lax.axis_index("head")
    length = tokens.shape[1]
    score_scale = 1.0 / math.sqrt(HD)
    pack = jnp.concatenate(
        [
            lax.dynamic_slice_in_dim(w_keyval, 64 * h, 128, 1),
            lax.dynamic_slice_in_dim(w_keyval, 320 + 64 * h, 128, 1),
            w_query,
            w_out.T,
        ],
        axis=1,
    )
    weights, decode, stored = gather(pack, prior_cache)
    flat = tokens[0]
    normed = rms_norm(flat.astype(jnp.float32), attn_gain.astype(jnp.float32)).astype(jnp.bfloat16)
    first = jnp.dot(normed, weights[:, :576], preferred_element_type=jnp.float32)
    prior_count = lax.dynamic_index_in_dim(prior_len, seq_index, keepdims=False)
    stretch_count = lax.dynamic_index_in_dim(stretch_len, seq_index, keepdims=False)
    offsets = jnp.arange(length, dtype=jnp.int32)
    positions = prior_count + offsets
    query = rotary(
        rms_norm(first[:, 256:].reshape(length, 5, HD), q_gain.astype(jnp.float32)), positions
    ).astype(jnp.bfloat16)
    keys = rotary(
        rms_norm(first[:, :128].reshape(length, 2, HD), k_gain.astype(jnp.float32)), positions
    ).astype(jnp.bfloat16).reshape(length, 128)
    values = first[:, 128:256].astype(jnp.bfloat16)
    tiles = [stored[:, j].reshape(512, 128) for j in range(3)]
    even = h % 2 == 0
    k_prior = jnp.where(even, tiles[0], half_swap(tiles[0], tiles[1]))
    v_prior = jnp.where(even, half_swap(tiles[1], tiles[2]), tiles[2])
    all_keys = jnp.concatenate([k_prior, keys], axis=0)
    all_values = jnp.concatenate([v_prior, values], axis=0)
    which = (jnp.arange(5) >= 4 - h)
    lane_second = jnp.arange(128) >= 64
    spread = jnp.concatenate([query, query], axis=2)
    spread = jnp.where(which[None, :, None] == lane_second[None, None, :], spread, jnp.zeros_like(spread))
    scores = jnp.einsum("qhd,kd->hqk", spread, all_keys, preferred_element_type=jnp.float32) * score_scale
    earlier = jnp.arange(512, dtype=jnp.int32)[None, :] < prior_count
    allowed = jnp.concatenate(
        [jnp.broadcast_to(earlier, (length, 512)), offsets[None, :] <= offsets[:, None]], axis=1
    )
    scores = jnp.where(allowed[None], scores, -jnp.inf)
    top = jnp.max(scores, axis=-1, keepdims=True)
    w = jnp.exp(scores - top)
    total = jnp.sum(w, axis=-1)
    mixed = jnp.einsum("hqk,kd->qhd", w.astype(jnp.bfloat16), all_values, preferred_element_type=jnp.float32)
    mixed = jnp.where(which[None, :, None], mixed[..., 64:], mixed[..., :64]) / total.T[:, :, None]
    attended = mixed.astype(jnp.bfloat16).reshape(length, 320)
    terms = lax.dot_general(
        attended, weights[:, 576:], (((1,), (1,)), ((), ())), preferred_element_type=jnp.float32
    ).astype(jnp.bfloat16)
    got, kv = swap(terms.reshape(NY, 32, 2048), jnp.concatenate([keys, values], axis=1).reshape(NY, 32, 256))
    summed = jnp.sum(got.astype(jnp.float32), axis=0)
    own_tokens = lax.dynamic_slice_in_dim(flat, h * 32, 32, 0).astype(jnp.float32)
    residual = own_tokens + summed
    valid = (h * 32 + jnp.arange(32, dtype=jnp.int32))[:, None] < stretch_count
    hidden = jnp.where(valid, residual, 0.0).astype(jnp.bfloat16)
    ffn_input = jnp.where(valid, rms_norm(residual, ffn_gain.astype(jnp.float32)), 0.0).astype(jnp.bfloat16)
    fresh = jnp.concatenate(
        [kv[0][:, :128], kv[2][:, :128], kv[3][:, 64:128], kv[0][:, 128:192], kv[1][:, 128:], kv[3][:, 128:]], axis=1
    )
    fresh = jnp.where(valid, fresh, jnp.zeros_like(fresh))
    return (hidden[None], ffn_input[None], fresh[None], decode.reshape(1, 128, 640))


def solution(mesh):
    placed = (
        P("seq", None, None),
        P(),
        P(),
        P(),
        P(),
        P("seq", "head"),
        P("seq", None),
        P("head", "seq"),
        P(None, "seq", None),
        P(),
        P(),
    )
    return jax.shard_map(
        shards,
        mesh=mesh,
        in_specs=placed,
        out_specs=(
            P("seq", "head", None),
            P("seq", "head", None),
            P("seq", "head", None),
            P("seq", "head", None),
        ),
        check_vma=False,
    )
```

time: 475 us -> 94 us (0.20)
  waiting for transfers between devices: 414 us -> 0 us
  Pallas kernels: 0 us -> 69.9 us
  starting transfers between devices: 20.5 us -> 0 us
  between operations: 14.1 us -> 0.99 us
    all_gather x3 -> x0, waiting for transfers between devices: 359 us -> none  [the longest x1 136 us: shards(): lax.all_gather(w_keyval, 'seq', axis=0, tiled=True)]
    pallas_call x0 -> x2, Pallas kernels: none -> 69.9 us  [the longest x1 56.1 us: gather(): pl.pallas_call(gather_kernel, out_shape=(jax.ShapeDtypeStruct((2048, WIDE...]
    all_to_all x1 -> x0, waiting for transfers between devices: 32.9 us -> none  [shards(): lax.all_to_all(prior_cache, 'seq', split_axis=0, concat_axis=1, tiled=True)]
    all_to_all x1 -> x0, starting transfers between devices: 20.4 us -> none  [shards(): lax.all_to_all(prior_cache, 'seq', split_axis=0, concat_axis=1, tiled=True)]
    reduce_scatter x1 -> x0, waiting for transfers between devices: 20 us -> none  [shards(): lax.psum_scatter(terms.reshape(local_requests, length, width).astype(jnp....]
  transfers between devices with their start and end apart: 5 -> 0, of which waited for: 5 -> 0; matrix products, arithmetic and copies ran while one was open for 4% -> 0% of each run, Pallas kernels for 0% -> 0%
where the time goes in v1:
time: 94 us; the launch traced here: 93.5 us
  Pallas kernels  69.9 us (74%)
  other arithmetic  10.8 us (11%)
  matrix products  7.13 us (8%)
  local copies, waits for them, and re-layouts  4.69 us (5%)
  between operations  0.99 us (1%)
    pallas_call x1, Pallas kernels, gather(): pl.pallas_call(gather_kernel, out_shape=(jax.ShapeDtypeStruct((2048, WIDE...  56.1 us
    pallas_call x1, Pallas kernels, swap(): pl.pallas_call(swap_kernel, out_shape=(jax.ShapeDtypeStruct(terms.shape,...  13.8 us
    dot_general x1, matrix products, shards(): lax.dot_general(attended, weights[:, 576:], (((1,), (1,)), ((), ())), pre...  3.16 us
    dot_general x1, matrix products, shards(): jnp.dot(normed, weights[:, :576], preferred_element_type=jnp.float32)  3.08 us

profile of v1, /device:TPU:1, one launch (start us, length us, event | category | flops | bytes accessed | tf_op | source)
XLA Modules:
  0.0 93.5 jit_solution(1679685051174590058)
XLA Ops:
  0.6 0.8 constant_dynamic-slice_fusion.1
  1.4 1.4 %pad_maximum_fusion.3.pack_ref = bf16[16,896]{1,0:T(8,128)(2,1)} fusion(bf16[16,320]{1,0:T(8,128)(2,1)} %bitcast.96, bf16[16,320]{1,0:T(8,128)(2,1)} %param.16, bf16[16,128]{1,0:T(8,128)(2,1)S(1)} %get-tuple-element.30, bf16[16,128]{1,0:T(8,128)(2,1)S(1)} %get-tuple-element.29), kind=kLoop, calls=%fused_computation.66 | loop fusion | flops 114688 | bytes 57344 | tf_op jit(solution)/shard_map/concatenate | solution.py:315
  2.8 56.1 %gather.1 = (bf16[2048,896]{1,0:T(8,128)(2,1)}, bf16[32,4,640]{2,1,0:T(4,128)(2,1)}, bf16[4,3,32,4,128]{4,3,2,1,0:T(4,128)(2,1)}) custom-call(bf16[16,896]{1,0:T(8,128)(2,1)} %pad_maximum_fusion.3.pack_ref, bf16[128,4,640]{2,1,0:T(4,128)(2,1)} %cache_ref.1), custom_call_target="tpu_custom_call" | custom-call | tf_op jit(solution)/shard_map/gather/pallas_call | solution.py:238
  58.9 0.7 convert_element_type.70
  59.6 1.2 %fusion.5 = f32[128]{0:T(128)S(1)} fusion(bf16[1,128,2048]{2,1,0:T(8,128)(2,1)} %param.11), kind=kLoop, calls=%fused_computation.11 | loop fusion | flops 786304 | bytes 524800 | tf_op jit(solution)/shard_map/reduce_sum | solution.py:22
  60.9 3.1 %fusion = f32[128,576]{0,1:T(8,128)S(1)} fusion(bf16[2048,896]{1,0:T(8,128)(2,1)} %get-tuple-element.10, bf16[1,128,2048]{2,1,0:T(8,128)(2,1)} %param.11, f32[2048]{0:T(1024)S(1)} %convert_element_type.70, f32[128]{0:T(128)S(1)} %add_rsqrt_fusion.3), kind=kOutput, calls=%fused_computation | convolution fusion | flops 303038464 | bytes 3449344 | tf_op jit(solution)/shard_map/dot_general | solution.py:327
  64.1 0.6 dynamic_slice.20
  64.7 0.6 add_convert_fusion
  65.4 0.3 multiply_cosine_fusion
  66.3 0.1 copy.15
  66.4 0.6 pad_maximum_fusion.2.kv_ref
  67.1 0.2 fusion.34
  67.4 0.2 maximum_select_fusion.2
  67.7 0.2 copy.19
  67.9 0.2 multiply_multiply_fusion
  68.0 0.2 slice_negate_fusion
  68.2 0.2 fusion.15
  68.5 0.7 iota_compare_fusion.1
  69.2 0.1 pad_add_fusion
  69.4 0.5 fusion.36
  69.9 0.2 fusion.3
  70.1 0.4 convolution_bitcast_fusion
  70.7 3.2 %convolution_convert_fusion = bf16[128,2048]{1,0:T(8,128)(2,1)} fusion(bf16[128,320]{0,1:T(8,128)(2,1)S(1)} %bitcast.92, bf16[2048,896]{1,0:T(8,128)(2,1)} %get-tuple-element.10), kind=kOutput, calls=%fused_computation.2 | convolution fusion | flops 168034304 | bytes 2179072 | tf_op jit(solution)/shard_map/dot_general | solution.py:361
  73.8 13.8 %swap.1 = (bf16[4,32,2048]{2,1,0:T(8,128)(2,1)}, bf16[4,32,256]{2,1,0:T(8,128)(2,1)}) custom-call(bf16[4,32,2048]{2,1,0:T(8,128)(2,1)} %bitcast.84, bf16[4,32,256]{2,1,0:T(8,128)(2,1)} %pad_maximum_fusion.2.kv_ref), custom_call_target="tpu_custom_call" | custom-call | tf_op jit(solution)/shard_map/swap/pallas_call | solution.py:292
  87.7 0.8 slice_bitcast_fusion
  88.7 0.6 dynamic_slice.16
  89.3 0.7 add_compare_fusion
  89.9 0.7 broadcast_select_fusion
  90.6 1.1 %convert_reduce_fusion = f32[32,2048]{1,0:T(8,128)S(1)} fusion(bf16[4,32,2048]{2,1,0:T(8,128)(2,1)} %get-tuple-element.11), kind=kLoop, calls=%fused_computation.14 | loop fusion | flops 458752 | bytes 786432 | tf_op jit(solution)/shard_map/reduce_sum | solution.py:365
  91.8 0.2 fusion.18
  91.9 0.8 select_convert_fusion
  92.8 0.7 reshape.266
  (53 shorter events, 1.4 us)
Async XLA Ops:
  60.8 3.2 %copy-start.5 = (bf16[64]{0:T(256)(128)(2,1)S(1)}, bf16[64]{0:T(256)(128)(2,1)}, u32[]{:S(2)}) copy-start(bf16[64]{0:T(256)(128)(2,1)} %param.14) | copy-start | bytes 388
  60.8 3.3 %copy-start.4 = (s32[128]{0:T(128)S(1)}, s32[128]{0:T(128)}, u32[]{:S(2)}) copy-start(s32[128]{0:T(128)} %param.20) | copy-start | bytes 1540
  63.9 3.1 %copy-start.1 = (bf16[4,3,32,4,128]{4,3,2,1,0:T(4,128)(2,1)S(1)}, bf16[4,3,32,4,128]{4,3,2,1,0:T(4,128)(2,1)}, u32[]{:S(2)}) copy-start(bf16[4,3,32,4,128]{4,3,2,1,0:T(4,128)(2,1)} %get-tuple-element.9) | copy-start | bytes 1179652
  67.1 0.8 copy-start.6
  70.7 18.0 %copy-start.7 = (s32[128]{0:T(128)S(1)}, s32[128]{0:T(128)}, u32[]{:S(2)}) copy-start(s32[128]{0:T(128)} %param.21) | copy-start | bytes 1540
  70.7 21.1 %copy-start = (bf16[1,128,2048]{2,1,0:T(8,128)(2,1)S(1)}, bf16[1,128,2048]{2,1,0:T(8,128)(2,1)}, u32[]{:S(2)}) copy-start(bf16[1,128,2048]{2,1,0:T(8,128)(2,1)} %param.11) | copy-start | bytes 1572868
  73.8 18.1 %copy-start.3 = (bf16[2048]{0:T(1024)(128)(2,1)S(1)}, bf16[2048]{0:T(1024)(128)(2,1)}, u32[]{:S(2)}) copy-start(bf16[2048]{0:T(1024)(128)(2,1)} %param.15) | copy-start | bytes 12292
  73.8 18.9 %copy-start.2 = (bf16[32,4,640]{2,1,0:T(4,128)(2,1)S(1)}, bf16[32,4,640]{2,1,0:T(4,128)(2,1)}, u32[]{:S(2)}) copy-start(bf16[32,4,640]{2,1,0:T(4,128)(2,1)} %get-tuple-element.13) | copy-start | bytes 491524

commit v2 on v0

v2 whole, which is shorter than its diff:
```python
import math

import jax
import jax.numpy as jnp
from jax import lax
from jax.experimental import pallas as pl
from jax.experimental.pallas import tpu as pltpu
from jax.sharding import PartitionSpec as P

HD = 64
NX, NZ, NY = 4, 16, 4
PLANE = NZ * 2
A, B = 640, 256
MESH = pl.DeviceIdType.MESH
BF = jnp.bfloat16
F32 = jnp.float32
epsilon = 1e-06


def body(
    tok, again, qgain, kgain, fgain, wq, wkv, wo, cache, cosine, sine, prior, stretch,
    hidden, ffn, fresh, decode,
    wa, wb, cpack, xb, eb, yb, normed, acc, qs, kvs, kvr, tb, rb,
    a_send, a_recv, b_send, b_recv, x_send, x_recv, e_send, e_recv, y_send, y_recv, k_send, k_recv, t_send, t_recv,
):
    s = lax.axis_index("seq")
    h = lax.axis_index("head")
    x = s // PLANE
    low = lax.rem(s, PLANE)
    z = low // 2
    c = lax.rem(low, 2)

    def sid(xx, zz, cc):
        return xx * PLANE + zz * 2 + cc

    def wrapx(v):
        return lax.rem(v + NX, NX)

    def wrapz(v):
        return lax.rem(v + NZ, NZ)

    barrier = pltpu.get_barrier_semaphore()

    def signal(target):
        pl.semaphore_signal(barrier, inc=1, device_id=target, device_id_type=MESH)

    def greet(k, carry):
        signal({"seq": x * PLANE + lax.rem(low + k, PLANE)})
        return carry

    lax.fori_loop(1, PLANE, greet, 0)
    for k in range(1, NX):
        signal({"seq": sid(wrapx(x + k), z, c)})
    for k in range(1, NY):
        signal({"head": lax.rem(h + k, NY)})

    own = pl.ds(pl.multiple_of(s * 16, 16), 16)
    for head in range(NY):

        @pl.when(h == head)
        def _(head=head):
            lo = 64 * head
            wa[own, 0:128] = wkv[:, lo : lo + 128]
            wa[own, 128:256] = wkv[:, 320 + lo : 448 + lo]

            def pack(i, carry):
                at = pl.ds(pl.multiple_of(i * 16, 16), 16)
                cpack[at, :, 0:128] = cache[at, :, lo : lo + 128]
                cpack[at, :, 128:256] = cache[at, :, 320 + lo : 448 + lo]
                return carry

            lax.fori_loop(0, 8, pack, 0)

    wa[own, 256:640] = jnp.concatenate([wq[...], wo[:, 0:64]], axis=1)
    wb[own, :] = wo[:, 64:320]

    def norm(i, carry):
        at = pl.ds(pl.multiple_of(i * 16, 16), 16)
        v = tok[at, :].astype(F32)
        v = v * lax.rsqrt(jnp.mean(v * v, axis=-1, keepdims=True) + epsilon) * again[...]
        normed[at, :] = v.astype(BF)
        return carry

    lax.fori_loop(0, 8, norm, 0)
    pl.semaphore_wait(barrier, PLANE - 1 + NX - 1 + NY - 1)

    ahead = jnp.where(c == 0, 1, -1)
    partner = {"seq": sid(x, z, 1 - c)}

    def tox(d):
        return {"seq": sid(wrapx(x + d), z, c)}

    def toz(d):
        return {"seq": sid(x, wrapz(z + d), c)}

    class Ring:
        def __init__(self, buf, send, recv):
            self.buf, self.send, self.recv, self.count = buf, send, recv, 0

        def rows(self, b):
            return self.buf.at[pl.ds(pl.multiple_of(b * 16, 16), 16)]

        def push(self, b, target):
            self.count += 1
            pltpu.make_async_remote_copy(
                src_ref=self.rows(b),
                dst_ref=self.rows(b),
                send_sem=self.send,
                recv_sem=self.recv.at[b],
                device_id=target,
                device_id_type=MESH,
            ).start()

        def arrive(self, b):
            pltpu.make_async_copy(self.rows(b), self.rows(b), self.recv.at[b]).wait()

        def spread(self, b):
            self.push(b, tox(ahead))
            self.push(b, tox(-ahead))
            self.push(b, partner)

        def near(self, b):
            for d in (2, 1, -1):
                self.push(b, toz(d))

        def start(self):
            for d in (8, 4, -4):
                self.push(s, toz(d))
            self.near(s)
            self.spread(s)

        def here(self, d, far=False):
            b = sid(x, wrapz(z + d), c)
            self.arrive(b)
            if far:
                self.near(b)
            self.spread(b)

        def relay(self, d):
            b = sid(wrapx(x - ahead), wrapz(z + d), c)
            self.arrive(b)
            self.push(b, tox(ahead))
            self.push(b, partner)
            b = sid(wrapx(x + ahead), wrapz(z + d), c)
            self.arrive(b)
            self.push(b, partner)

        def last(self, d):
            b = sid(wrapx(x + 2), wrapz(z + d), c)
            self.arrive(b)
            self.push(b, partner)

        def shared(self, xx):
            def one(zz, carry):
                self.arrive(sid(xx, zz, 1 - c))
                return carry

            lax.fori_loop(0, NZ, one, 0)

        def drain(self):
            left = self.count
            while left > 0:
                n = min(left, 128)
                part = self.buf.at[pl.ds(0, n * 16)]
                pltpu.make_async_copy(part, part, self.send).wait()
                left -= n

    ra, rbq = Ring(wa, a_send, a_recv), Ring(wb, b_send, b_recv)
    ra.start()
    for k in (2, 1, 3):
        xx = wrapx(x + k)
        pltpu.make_async_remote_copy(
            src_ref=cpack.at[pl.ds(pl.multiple_of(xx * PLANE, PLANE), PLANE)],
            dst_ref=xb.at[x],
            send_sem=x_send,
            recv_sem=x_recv,
            device_id=tox(k),
            device_id_type=MESH,
        ).start()
    pltpu.make_async_copy(cpack.at[pl.ds(pl.multiple_of(x * PLANE, PLANE), PLANE)], xb.at[x], x_recv).start()
    near, far = (-1, 1, -2), (-4, 4, 8)
    rest = (-5, -3, 3, 5, -6, 2, 7, -7, 6)
    rbq.start()
    for d in near:
        ra.here(d)
    for d in far:
        ra.here(d, True)
    pltpu.make_async_copy(xb, xb, x_recv).wait()

    def hand(k, carry):
        to = lax.rem(low + k, PLANE)
        pltpu.make_async_remote_copy(
            src_ref=xb.at[:, to],
            dst_ref=eb.at[:, low],
            send_sem=e_send,
            recv_sem=e_recv,
            device_id={"seq": x * PLANE + to},
            device_id_type=MESH,
        ).start()
        return carry

    lax.fori_loop(1, PLANE, hand, 0)
    pltpu.make_async_copy(xb.at[:, low], eb.at[:, low], e_recv).start()
    ra.relay(0)
    for d in near:
        ra.relay(d)
    ra.last(0)
    for d in rest[:4]:
        ra.here(d)
    for d in near:
        rbq.here(d)
    for d in far:
        rbq.here(d, True)
    for d in rest[4:]:
        ra.here(d)
    for d in far:
        ra.relay(d)
    for d in near:
        ra.last(d)
    for d in rest[:4]:
        ra.relay(d)
    rbq.relay(0)
    for d in near:
        rbq.relay(d)
    for d in far:
        ra.last(d)
    for d in rest[4:]:
        ra.relay(d)
    ra.shared(x)

    def project(xx, first=False):
        deep = pl.ds(pl.multiple_of(xx * 512, 512), 512)
        part = jnp.dot(normed[:, deep], wa[deep, :], preferred_element_type=F32)
        if first:
            acc[...] = part
        else:
            acc[...] += part

    project(x, True)
    for d in rest:
        ra.last(d)
    for d in rest:
        rbq.here(d)
    ra.shared(wrapx(x + 1))
    project(wrapx(x + 1))
    ra.shared(wrapx(x - 1))
    project(wrapx(x - 1))
    rbq.last(0)
    for d in far:
        rbq.relay(d)
    for d in near:
        rbq.last(d)
    ra.shared(wrapx(x + 2))
    project(wrapx(x + 2))
    for d in rest:
        rbq.relay(d)

    lane = lax.broadcasted_iota(jnp.int32, (128, 128), 1)
    row = lax.broadcasted_iota(jnp.int32, (128, 128), 0)
    upper = lane >= 64
    flip = lax.rem(lane, 64) < 32

    def position(t, gain):
        sq = t * t
        lo = jnp.sum(jnp.where(upper, 0.0, sq), axis=-1, keepdims=True)
        hi = jnp.sum(jnp.where(upper, sq, 0.0), axis=-1, keepdims=True)
        v = t * lax.rsqrt(jnp.where(upper, hi, lo) * (1.0 / 64) + epsilon) * gain
        turned = jnp.where(flip, pltpu.roll(v, 96, 1), pltpu.roll(v, 32, 1))
        return v * cosine[...] + turned * sine[...]

    keys = position(acc[:, 0:128], kgain[...]).astype(BF)
    values = acc[:, 128:256].astype(BF)
    kvs[:, :, 0:128] = keys.reshape(NY, 32, 128)
    kvs[:, :, 128:256] = values.reshape(NY, 32, 128)
    kvr[h] = kvs[h]
    for k in (2, 1, 3):
        to = lax.rem(h + k, NY)
        pltpu.make_async_remote_copy(
            src_ref=kvs.at[to],
            dst_ref=kvr.at[h],
            send_sem=k_send,
            recv_sem=k_recv,
            device_id={"head": to},
            device_id_type=MESH,
        ).start()
    second = [jnp.where(i >= 4 - h, 1, 0) for i in range(5)]
    for pair in range(3):
        t = position(acc[:, 256 + 128 * pair : 384 + 128 * pair], qgain[...])
        r = pltpu.roll(t, 64, 1)
        for half in range(2):
            i = 2 * pair + half
            if i < 5:
                v = jnp.where(second[i] == half, t, r)
                v = jnp.where(jnp.where(upper, 1, 0) == second[i], v, 0.0)
                qs[128 * i : 128 * (i + 1), :] = v.astype(BF)

    pltpu.make_async_copy(eb, eb, e_recv).wait()
    for k in (2, 1, 3):
        to = lax.rem(h + k, NY)
        pltpu.make_async_remote_copy(
            src_ref=eb.at[to],
            dst_ref=yb.at[h],
            send_sem=y_send,
            recv_sem=y_recv,
            device_id={"head": to},
            device_id_type=MESH,
        ).start()
    pltpu.make_async_copy(eb.at[h], yb.at[h], y_recv).start()
    stored = [eb[p].reshape(128, 256) for p in range(4)]
    all_keys = jnp.concatenate([t[:, 0:128] for t in stored] + [keys], axis=0)
    all_values = jnp.concatenate([t[:, 128:256] for t in stored] + [values], axis=0)
    prior_count = prior[s]
    slot = lax.broadcasted_iota(jnp.int32, (128, 512), 1)
    earlier = slot < prior_count
    causal = lane <= row
    allowed = jnp.concatenate([earlier, causal], axis=1)
    heads = []
    for i in range(5):
        sc = lax.dot_general(
            qs[128 * i : 128 * (i + 1), :], all_keys, (((1,), (1,)), ((), ())), preferred_element_type=F32
        ) * (1.0 / math.sqrt(HD))
        sc = jnp.where(allowed, sc, -jnp.inf)
        w = jnp.exp(sc - jnp.max(sc, axis=-1, keepdims=True))
        total = jnp.sum(w, axis=-1, keepdims=True)
        m = jnp.dot(w.astype(BF), all_values, preferred_element_type=F32) / total
        heads.append(jnp.where(second[i] == (i + 1) % 2, m, pltpu.roll(m, 64, 1)))
    att = [
        jnp.where(upper, heads[0], 0.0).astype(BF),
        jnp.where(upper, heads[2], heads[1]).astype(BF),
        jnp.where(upper, heads[4], heads[3]).astype(BF),
    ]
    att12 = jnp.concatenate(att[1:], axis=1)

    def project_out(xx):
        wide = pl.ds(pl.multiple_of(xx * 512, 512), 512)
        dims = (((1,), (1,)), ((), ()))
        part = lax.dot_general(att[0], wa[wide, 512:640], dims, preferred_element_type=F32)
        part = part + lax.dot_general(att12, wb[wide, :], dims, preferred_element_type=F32)
        tb[:, :, wide] = part.astype(BF).reshape(NY, 32, 512)
        for k in (2, 1, 3):
            to = lax.rem(h + k, NY)
            pltpu.make_async_remote_copy(
                src_ref=tb.at[to, :, wide],
                dst_ref=rb.at[h, :, wide],
                send_sem=t_send,
                recv_sem=t_recv,
                device_id={"head": to},
                device_id_type=MESH,
            ).start()

    rbq.shared(x)
    project_out(x)
    for d in far + rest:
        rbq.last(d)
    for d in (1, -1, 2):
        rbq.shared(wrapx(x + d))
        project_out(wrapx(x + d))

    limit = stretch[s]

    def assemble(t0, t1, t2, t3):
        low_half = lax.broadcasted_iota(jnp.int32, (t0.shape[0], 128), 1) < 64
        mid = pltpu.roll(jnp.where(low_half, t0[:, 128:256].astype(F32), t3[:, 0:128].astype(F32)), 64, 1).astype(BF)
        return jnp.concatenate([t0[:, 0:128], t2[:, 0:128], mid, t1[:, 128:256], t3[:, 128:256]], axis=1)

    pltpu.make_async_copy(yb, yb, y_recv).wait()
    decode[...] = assemble(*[yb[p].reshape(128, 256) for p in range(4)])
    three = kvr.at[pl.ds(0, 3)]
    pltpu.make_async_copy(three, three, k_recv).wait()
    rows = h * 32 + lax.broadcasted_iota(jnp.int32, (32, 640), 0)
    made = assemble(*[kvr[p] for p in range(4)])
    fresh[...] = jnp.where(rows < limit, made, jnp.zeros_like(made))

    three = rb.at[pl.ds(0, 3)]
    pltpu.make_async_copy(three, three, t_recv).wait()
    summed = tok[pl.ds(pl.multiple_of(h * 32, 32), 32), :].astype(F32)
    share = tb[h].astype(F32)
    for k in range(1, NY):
        share = share + rb[lax.rem(h + k, NY)].astype(F32)
    resid = summed + share
    valid = h * 32 + lax.broadcasted_iota(jnp.int32, (32, 2048), 0) < limit
    hidden[...] = jnp.where(valid, resid, 0.0).astype(BF)
    scaled = resid * lax.rsqrt(jnp.mean(resid * resid, axis=-1, keepdims=True) + epsilon) * fgain[...]
    ffn[...] = jnp.where(valid, scaled, 0.0).astype(BF)

    for ref, sem in ((xb.at[pl.ds(0, 3)], x_send), (eb.at[:, pl.ds(0, PLANE - 1)], e_send),
                     (yb.at[pl.ds(0, 3)], y_send), (kvr.at[pl.ds(0, 3)], k_send), (rb.at[pl.ds(0, 3)], t_send)):
        pltpu.make_async_copy(ref, ref, sem).wait()
    ra.drain()
    rbq.drain()


def block(*args):
    vmem = pl.BlockSpec(memory_space=pltpu.VMEM)
    smem = pl.BlockSpec(memory_space=pltpu.SMEM)
    dma = pltpu.SemaphoreType.DMA
    many = pltpu.SemaphoreType.DMA((NX * PLANE,))
    cache_like = pltpu.VMEM((NX, PLANE, 4, 256), BF)
    return pl.pallas_call(
        body,
        out_shape=(
            jax.ShapeDtypeStruct((32, 2048), BF),
            jax.ShapeDtypeStruct((32, 2048), BF),
            jax.ShapeDtypeStruct((32, 640), BF),
            jax.ShapeDtypeStruct((128, 640), BF),
        ),
        in_specs=[vmem] * 11 + [smem] * 2,
        out_specs=(vmem,) * 4,
        scratch_shapes=[
            pltpu.VMEM((2048, A), BF),
            pltpu.VMEM((2048, B), BF),
            pltpu.VMEM((128, 4, 256), BF),
            cache_like,
            cache_like,
            cache_like,
            pltpu.VMEM((128, 2048), BF),
            pltpu.VMEM((128, A), F32),
            pltpu.VMEM((640, 128), BF),
            pltpu.VMEM((NY, 32, 256), BF),
            pltpu.VMEM((NY, 32, 256), BF),
            pltpu.VMEM((NY, 32, 2048), BF),
            pltpu.VMEM((NY, 32, 2048), BF),
            dma, many, dma, many, dma, dma, dma, dma, dma, dma, dma, dma, dma, dma,
        ],
        compiler_params=pltpu.CompilerParams(collective_id=0, has_side_effects=True),
        name="block",
    )(*args)


def shards(tokens, attn_gain, q_gain, k_gain, ffn_gain, w_query, w_keyval, w_out, prior_cache, prior_len, stretch_len):
    seq_index = lax.axis_index("seq")
    length = tokens.shape[1]
    prior_count = lax.dynamic_index_in_dim(prior_len, seq_index, keepdims=False)
    positions = (prior_count + jnp.arange(length, dtype=jnp.int32)).astype(F32)
    middle = HD // 2
    inverse = jnp.exp(jnp.arange(middle, dtype=F32) * (-2.0 * math.log(10000.0) / HD))
    angles = positions[:, None] * inverse[None, :]
    cosine, sine = jnp.cos(angles), jnp.sin(angles)
    cosine = jnp.concatenate([cosine] * 4, axis=1)
    sine = jnp.concatenate([-sine, sine, -sine, sine], axis=1)

    def twice(gain):
        return jnp.concatenate([gain, gain])[None].astype(F32)

    hidden, ffn, fresh, decode = block(
        tokens[0],
        attn_gain[None].astype(F32),
        twice(q_gain),
        twice(k_gain),
        ffn_gain[None].astype(F32),
        w_query,
        w_keyval,
        w_out.T,
        prior_cache,
        cosine,
        sine,
        prior_len,
        stretch_len,
    )
    return (hidden[None], ffn[None], fresh[None], decode[None])


def solution(mesh):
    placed = (
        P("seq", None, None),
        P(),
        P(),
        P(),
        P(),
        P("seq", "head"),
        P("seq", None),
        P("head", "seq"),
        P(None, "seq", None),
        P(),
        P(),
    )
    return jax.shard_map(
        shards,
        mesh=mesh,
        in_specs=placed,
        out_specs=(P("seq", "head", None),) * 4,
        check_vma=False,
    )
```

time: 475 us -> 71 us (0.15)
  waiting for transfers between devices: 414 us -> 0 us
  Pallas kernels: 0 us -> 60.4 us
  starting transfers between devices: 20.5 us -> 0 us
  between operations: 14.1 us -> 0.71 us
  matrix products: 7.37 us -> 0 us
  other arithmetic: 8.47 us -> 3.63 us
    all_gather x3 -> x0, waiting for transfers between devices: 359 us -> none  [the longest x1 136 us: shards(): lax.all_gather(w_keyval, 'seq', axis=0, tiled=True)]
    pallas_call x0 -> x1, Pallas kernels: none -> 60.4 us  [block(): pl.pallas_call(body, out_shape=(jax.ShapeDtypeStruct((32, 2048), BF), jax...]
    all_to_all x1 -> x0, waiting for transfers between devices: 32.9 us -> none  [shards(): lax.all_to_all(prior_cache, 'seq', split_axis=0, concat_axis=1, tiled=True)]
    all_to_all x1 -> x0, starting transfers between devices: 20.4 us -> none  [shards(): lax.all_to_all(prior_cache, 'seq', split_axis=0, concat_axis=1, tiled=True)]
    reduce_scatter x1 -> x0, waiting for transfers between devices: 20 us -> none  [shards(): lax.psum_scatter(terms.reshape(local_requests, length, width).astype(jnp....]
    dot_general x5 -> x0, matrix products: 7.37 us -> none  [the longest x1 2.92 us: shards(): jnp.dot(normed, lax.all_gather(w_keyval, 'seq', axis=0, tiled=True), pref...]
  transfers between devices with their start and end apart: 5 -> 0, of which waited for: 5 -> 0; matrix products, arithmetic and copies ran while one was open for 4% -> 0% of each run, Pallas kernels for 0% -> 0%
where the time goes in v2:
time: 71 us; the launch traced here: 70.4 us
  Pallas kernels  60.4 us (85%)
  local copies, waits for them, and re-layouts  5.63 us (8%)
  other arithmetic  3.63 us (5%)
  between operations  0.71 us (1%)
    pallas_call x1, Pallas kernels, block(): pl.pallas_call(body, out_shape=(jax.ShapeDtypeStruct((32, 2048), BF), jax...  60.4 us
    unnamed x20, local copies, waits for them, and re-layouts  5.05 us

profile of v2, /device:TPU:1, one launch (start us, length us, event | category | flops | bytes accessed | tf_op | source)
XLA Modules:
  0.0 70.4 jit_solution(1947680822963209812)
XLA Ops:
  0.6 0.0 copy-start.5
  0.6 0.6 copy-done.5
  1.3 0.6 dynamic_slice.4
  1.9 0.6 add_convert_fusion
  2.5 0.0 copy-start.6
  2.5 0.0 copy-start.7
  2.6 0.0 copy-start.3
  2.6 0.6 copy-done.6
  3.2 0.0 copy-done.7
  3.2 0.6 maximum_convert_fusion
  3.8 0.0 copy-done.3
  3.8 0.0 copy-start.4
  3.8 0.6 convert_element_type.30
  4.5 0.1 copy-done.4
  4.5 0.6 convert_element_type.31
  5.1 0.3 fusion
  5.5 0.8 %pad_maximum_fusion = (f32[128,128]{1,0:T(8,128)}, f32[128,128]{1,0:T(8,128)}) fusion(f32[128,32]{1,0:T(8,128)S(1)} %get-tuple-element.14, f32[128,32]{1,0:T(8,128)S(1)} %get-tuple-element.13, f32[128,32]{1,0:T(8,128)S(1)} %get-tuple-element.12), kind=kLoop, calls=%fused_computation.2 | loop fusion | flops 98304 | bytes 180224 | tf_op jit(solution)/shard_map/concatenate | solution.py:439
  6.3 60.4 %block.1 = (bf16[32,2048]{1,0:T(8,128)(2,1)}, bf16[32,2048]{1,0:T(8,128)(2,1)}, bf16[32,640]{1,0:T(8,128)(2,1)}, bf16[128,640]{1,0:T(8,128)(2,1)}) custom-call(bf16[128,2048]{1,0:T(8,128)(2,1)} %bitcast.11, f32[1,2048]{1,0:T(1,128)} %bitcast.16, f32[1,128]{1,0:T(1,128)} %get-tuple-element.17.qgain, f32[1,128]{1,0:T(1,128)} %get-tuple-element.18.kgain, ...), custom_call_target="tpu_custom_call" | custom-call | tf_op jit(solution)/shard_map/block/pallas_call | solution.py:399
  66.7 0.0 copy-start.1
  66.7 1.6 %copy.20 = bf16[1,32,2048]{2,1,0:T(8,128)(2,1)} copy(bf16[1,32,2048]{2,1,0:T(8,128)(2,1)} %bitcast.14) | data formatting | bytes 262144
  68.3 0.0 copy-done.1
  68.3 0.0 copy-start.2
  68.3 0.0 copy-start
  68.3 0.7 copy.21
  69.0 0.1 copy-done.2
  69.1 0.6 copy.22
  69.7 0.0 copy-done
  69.7 0.7 copy.23
  (1 shorter events, 0.0 us)
Async XLA Ops:
  0.6 0.7 copy-start.5
  2.5 0.7 copy-start.6
  2.5 0.7 copy-start.7
  2.6 1.3 %copy-start.3 = (bf16[2048]{0:T(1024)(128)(2,1)S(1)}, bf16[2048]{0:T(1024)(128)(2,1)}, u32[]{:S(2)}) copy-start(bf16[2048]{0:T(1024)(128)(2,1)} %param.12) | copy-start | bytes 12292
  3.8 0.7 copy-start.4
  66.7 1.6 %copy-start.1 = (bf16[32,2048]{1,0:T(8,128)(2,1)S(1)}, bf16[32,2048]{1,0:T(8,128)(2,1)}, u32[]{:S(2)}) copy-start(bf16[32,2048]{1,0:T(8,128)(2,1)} %get-tuple-element.9) | copy-start | bytes 393220
  68.3 0.8 %copy-start.2 = (bf16[32,640]{1,0:T(8,128)(2,1)S(1)}, bf16[32,640]{1,0:T(8,128)(2,1)}, u32[]{:S(2)}) copy-start(bf16[32,640]{1,0:T(8,128)(2,1)} %get-tuple-element.10) | copy-start | bytes 122884
  68.3 1.4 %copy-start = (bf16[128,640]{1,0:T(8,128)(2,1)S(1)}, bf16[128,640]{1,0:T(8,128)(2,1)}, u32[]{:S(2)}) copy-start(bf16[128,640]{1,0:T(8,128)(2,1)} %get-tuple-element.11) | copy-start | bytes 491524

commit v3 on v2

--- a/solution.py
+++ b/solution.py
@@ -18,9 +18,9 @@
 
 
 def body(
-    tok, again, qgain, kgain, fgain, wq, wkv, wo, cache, cosine, sine, prior, stretch,
+    tok, again, qgain, kgain, fgain, wq, wkv, wo, cache, prior, stretch,
     hidden, ffn, fresh, decode,
-    wa, wb, cpack, xb, eb, yb, normed, acc, qs, kvs, kvr, tb, rb,
+    wa, wb, cpack, xb, eb, yb, normed, acc, qs, kvs, kvr, tb, rb, cosine, sine,
     a_send, a_recv, b_send, b_recv, x_send, x_recv, e_send, e_recv, y_send, y_recv, k_send, k_recv, t_send, t_recv,
 ):
     s = lax.axis_index("seq")
@@ -63,25 +63,9 @@
             wa[own, 0:128] = wkv[:, lo : lo + 128]
             wa[own, 128:256] = wkv[:, 320 + lo : 448 + lo]
 
-            def pack(i, carry):
-                at = pl.ds(pl.multiple_of(i * 16, 16), 16)
-                cpack[at, :, 0:128] = cache[at, :, lo : lo + 128]
-                cpack[at, :, 128:256] = cache[at, :, 320 + lo : 448 + lo]
-                return carry
-
-            lax.fori_loop(0, 8, pack, 0)
-
     wa[own, 256:640] = jnp.concatenate([wq[...], wo[:, 0:64]], axis=1)
     wb[own, :] = wo[:, 64:320]
 
-    def norm(i, carry):
-        at = pl.ds(pl.multiple_of(i * 16, 16), 16)
-        v = tok[at, :].astype(F32)
-        v = v * lax.rsqrt(jnp.mean(v * v, axis=-1, keepdims=True) + epsilon) * again[...]
-        normed[at, :] = v.astype(BF)
-        return carry
-
-    lax.fori_loop(0, 8, norm, 0)
     pl.semaphore_wait(barrier, PLANE - 1 + NX - 1 + NY - 1)
 
     ahead = jnp.where(c == 0, 1, -1)
@@ -120,11 +104,11 @@
             self.push(b, partner)
 
         def near(self, b):
-            for d in (2, 1, -1):
+            for d in (2, -2, 1, -1):
                 self.push(b, toz(d))
 
         def start(self):
-            for d in (8, 4, -4):
+            for d in (5, -5, 8):
                 self.push(s, toz(d))
             self.near(s)
             self.spread(s)
@@ -167,6 +151,27 @@
 
     ra, rbq = Ring(wa, a_send, a_recv), Ring(wb, b_send, b_recv)
     ra.start()
+    for head in range(NY):
+
+        @pl.when(h == head)
+        def _(head=head):
+            lo = 64 * head
+
+            def pack(i, carry):
+                at = pl.ds(pl.multiple_of(i * 16, 16), 16)
+                cpack[at, :, 0:128] = cache[at, :, lo : lo + 128]
+                cpack[at, :, 128:256] = cache[at, :, 320 + lo : 448 + lo]
+                return carry
+
+            lax.fori_loop(0, 8, pack, 0)
+
+    prior_count = prior[s]
+    pair_lane = lax.rem(lax.broadcasted_iota(jnp.int32, (128, 128), 1), 64)
+    inverse = jnp.exp(lax.rem(pair_lane, 32).astype(F32) * (-2.0 * math.log(10000.0) / HD))
+    angles = (prior_count + lax.broadcasted_iota(jnp.int32, (128, 128), 0)).astype(F32) * inverse
+    cosine[...] = jnp.cos(angles)
+    sines = jnp.sin(angles)
+    sine[...] = jnp.where(pair_lane < 32, -sines, sines)
     for k in (2, 1, 3):
         xx = wrapx(x + k)
         pltpu.make_async_remote_copy(
@@ -178,11 +183,19 @@
             device_id_type=MESH,
         ).start()
     pltpu.make_async_copy(cpack.at[pl.ds(pl.multiple_of(x * PLANE, PLANE), PLANE)], xb.at[x], x_recv).start()
-    near, far = (-1, 1, -2), (-4, 4, 8)
-    rest = (-5, -3, 3, 5, -6, 2, 7, -7, 6)
-    rbq.start()
+    def norm(i, carry):
+        at = pl.ds(pl.multiple_of(i * 16, 16), 16)
+        v = tok[at, :].astype(F32)
+        v = v * lax.rsqrt(jnp.mean(v * v, axis=-1, keepdims=True) + epsilon) * again[...].astype(F32)[None, :]
+        normed[at, :] = v.astype(BF)
+        return carry
+
+    lax.fori_loop(0, 8, norm, 0)
+    near, far = (1, -1, 2, -2), (5, -5)
+    rest = (4, -4, 6, -6, 3, -3, 7, -7)
     for d in near:
         ra.here(d)
+    ra.relay(0)
     for d in far:
         ra.here(d, True)
     pltpu.make_async_copy(xb, xb, x_recv).wait()
@@ -201,31 +214,27 @@
 
     lax.fori_loop(1, PLANE, hand, 0)
     pltpu.make_async_copy(xb.at[:, low], eb.at[:, low], e_recv).start()
-    ra.relay(0)
+    rbq.start()
     for d in near:
         ra.relay(d)
     ra.last(0)
-    for d in rest[:4]:
+    ra.here(8)
+    for d in rest:
         ra.here(d)
+    for d in far:
+        ra.relay(d)
+    for d in near:
+        ra.last(d)
     for d in near:
         rbq.here(d)
     for d in far:
         rbq.here(d, True)
-    for d in rest[4:]:
-        ra.here(d)
-    for d in far:
+    ra.relay(8)
+    for d in rest:
         ra.relay(d)
-    for d in near:
-        ra.last(d)
-    for d in rest[:4]:
-        ra.relay(d)
-    rbq.relay(0)
-    for d in near:
-        rbq.relay(d)
     for d in far:
         ra.last(d)
-    for d in rest[4:]:
-        ra.relay(d)
+    rbq.relay(0)
     ra.shared(x)
 
     def project(xx, first=False):
@@ -237,14 +246,18 @@
             acc[...] += part
 
     project(x, True)
+    ra.last(8)
     for d in rest:
         ra.last(d)
+    rbq.here(8)
     for d in rest:
         rbq.here(d)
     ra.shared(wrapx(x + 1))
     project(wrapx(x + 1))
     ra.shared(wrapx(x - 1))
     project(wrapx(x - 1))
+    for d in near:
+        rbq.relay(d)
     rbq.last(0)
     for d in far:
         rbq.relay(d)
@@ -252,6 +265,7 @@
         rbq.last(d)
     ra.shared(wrapx(x + 2))
     project(wrapx(x + 2))
+    rbq.relay(8)
     for d in rest:
         rbq.relay(d)
 
@@ -268,7 +282,11 @@
         turned = jnp.where(flip, pltpu.roll(v, 96, 1), pltpu.roll(v, 32, 1))
         return v * cosine[...] + turned * sine[...]
 
-    keys = position(acc[:, 0:128], kgain[...]).astype(BF)
+    def twice(gain):
+        g = gain[...].astype(F32)[None, :]
+        return jnp.concatenate([g, g], axis=1)
+
+    keys = position(acc[:, 0:128], twice(kgain)).astype(BF)
     values = acc[:, 128:256].astype(BF)
     kvs[:, :, 0:128] = keys.reshape(NY, 32, 128)
     kvs[:, :, 128:256] = values.reshape(NY, 32, 128)
@@ -285,7 +303,7 @@
         ).start()
     second = [jnp.where(i >= 4 - h, 1, 0) for i in range(5)]
     for pair in range(3):
-        t = position(acc[:, 256 + 128 * pair : 384 + 128 * pair], qgain[...])
+        t = position(acc[:, 256 + 128 * pair : 384 + 128 * pair], twice(qgain))
         r = pltpu.roll(t, 64, 1)
         for half in range(2):
             i = 2 * pair + half
@@ -309,7 +327,6 @@
     stored = [eb[p].reshape(128, 256) for p in range(4)]
     all_keys = jnp.concatenate([t[:, 0:128] for t in stored] + [keys], axis=0)
     all_values = jnp.concatenate([t[:, 128:256] for t in stored] + [values], axis=0)
-    prior_count = prior[s]
     slot = lax.broadcasted_iota(jnp.int32, (128, 512), 1)
     earlier = slot < prior_count
     causal = lane <= row
@@ -350,7 +367,7 @@
 
     rbq.shared(x)
     project_out(x)
-    for d in far + rest:
+    for d in far + (8,) + rest:
         rbq.last(d)
     for d in (1, -1, 2):
         rbq.shared(wrapx(x + d))
@@ -380,7 +397,7 @@
     resid = summed + share
     valid = h * 32 + lax.broadcasted_iota(jnp.int32, (32, 2048), 0) < limit
     hidden[...] = jnp.where(valid, resid, 0.0).astype(BF)
-    scaled = resid * lax.rsqrt(jnp.mean(resid * resid, axis=-1, keepdims=True) + epsilon) * fgain[...]
+    scaled = resid * lax.rsqrt(jnp.mean(resid * resid, axis=-1, keepdims=True) + epsilon) * fgain[...].astype(F32)[None, :]
     ffn[...] = jnp.where(valid, scaled, 0.0).astype(BF)
 
     for ref, sem in ((xb.at[pl.ds(0, 3)], x_send), (eb.at[:, pl.ds(0, PLANE - 1)], e_send),
@@ -404,7 +421,7 @@
             jax.ShapeDtypeStruct((32, 640), BF),
             jax.ShapeDtypeStruct((128, 640), BF),
         ),
-        in_specs=[vmem] * 11 + [smem] * 2,
+        in_specs=[vmem] * 9 + [smem] * 2,
         out_specs=(vmem,) * 4,
         scratch_shapes=[
             pltpu.VMEM((2048, A), BF),
@@ -420,6 +437,8 @@
             pltpu.VMEM((NY, 32, 256), BF),
             pltpu.VMEM((NY, 32, 2048), BF),
             pltpu.VMEM((NY, 32, 2048), BF),
+            pltpu.VMEM((128, 128), F32),
+            pltpu.VMEM((128, 128), F32),
             dma, many, dma, many, dma, dma, dma, dma, dma, dma, dma, dma, dma, dma,
         ],
         compiler_params=pltpu.CompilerParams(collective_id=0, has_side_effects=True),
@@ -427,37 +446,27 @@
     )(*args)
 
 
+def settle_body(*refs):
+    for src, dst in zip(refs[:4], refs[4:]):
+        dst[...] = src[...]
+
+
+def settle(*made):
+    vmem = pl.BlockSpec(memory_space=pltpu.VMEM)
+    return pl.pallas_call(
+        settle_body,
+        out_shape=[jax.ShapeDtypeStruct(v.shape, v.dtype) for v in made],
+        in_specs=[vmem] * 4,
+        out_specs=[vmem] * 4,
+        name="settle",
+    )(*made)
+
+
 def shards(tokens, attn_gain, q_gain, k_gain, ffn_gain, w_query, w_keyval, w_out, prior_cache, prior_len, stretch_len):
-    seq_index = lax.axis_index("seq")
-    length = tokens.shape[1]
-    prior_count = lax.dynamic_index_in_dim(prior_len, seq_index, keepdims=False)
-    positions = (prior_count + jnp.arange(length, dtype=jnp.int32)).astype(F32)
-    middle = HD // 2
-    inverse = jnp.exp(jnp.arange(middle, dtype=F32) * (-2.0 * math.log(10000.0) / HD))
-    angles = positions[:, None] * inverse[None, :]
-    cosine, sine = jnp.cos(angles), jnp.sin(angles)
-    cosine = jnp.concatenate([cosine] * 4, axis=1)
-    sine = jnp.concatenate([-sine, sine, -sine, sine], axis=1)
-
-    def twice(gain):
-        return jnp.concatenate([gain, gain])[None].astype(F32)
-
-    hidden, ffn, fresh, decode = block(
-        tokens[0],
-        attn_gain[None].astype(F32),
-        twice(q_gain),
-        twice(k_gain),
-        ffn_gain[None].astype(F32),
-        w_query,
-        w_keyval,
-        w_out.T,
-        prior_cache,
-        cosine,
-        sine,
-        prior_len,
-        stretch_len,
+    made = block(
+        tokens[0], attn_gain, q_gain, k_gain, ffn_gain, w_query, w_keyval, w_out.T, prior_cache, prior_len, stretch_len
     )
-    return (hidden[None], ffn[None], fresh[None], decode[None])
+    return tuple(v[None] for v in settle(*made))
 
 
 def solution(mesh):

time: 71 us -> 70.5 us (level)
  Pallas kernels: 60.4 us -> 69 us
  local copies, waits for them, and re-layouts: 5.63 us -> 0 us
  other arithmetic: 3.63 us -> 0 us
    pallas_call x1, Pallas kernels: 60.4 us -> 67.2 us  [block(): pl.pallas_call(body, out_shape=(jax.ShapeDtypeStruct((32, 2048), BF), jax...]
    unnamed x20 -> x0, local copies, waits for them, and re-layouts: 5.05 us -> none
    convert_element_type x4 -> x0, other arithmetic: 2.49 us -> none  [the longest x1 0.65 us: shards(): positions = (prior_count + jnp.arange(length, dtype=jnp.int32)).astype(F32)]
    pallas_call x0 -> x1, Pallas kernels: none -> 1.84 us  [settle(): pl.pallas_call(settle_body, out_shape=[jax.ShapeDtypeStruct(v.shape, v.dt...]
    concatenate x1 -> x0, other arithmetic: 0.83 us -> none  [shards(): cosine = jnp.concatenate([cosine] * 4, axis=1)]
where the time goes in v3:
time: 70.5 us; the launch traced here: 69.7 us
  Pallas kernels  69 us (98%)
    pallas_call x1, Pallas kernels, block(): pl.pallas_call(body, out_shape=(jax.ShapeDtypeStruct((32, 2048), BF), jax...  67.2 us
    pallas_call x1, Pallas kernels, settle(): pl.pallas_call(settle_body, out_shape=[jax.ShapeDtypeStruct(v.shape, v.dt...  1.84 us

profile of v3, /device:TPU:1, one launch (start us, length us, event | category | flops | bytes accessed | tf_op | source)
XLA Modules:
  0.0 69.7 jit_solution(1372810917978930277)
XLA Ops:
  0.6 67.2 %block.1 = (bf16[32,2048]{1,0:T(8,128)(2,1)}, bf16[32,2048]{1,0:T(8,128)(2,1)}, bf16[32,640]{1,0:T(8,128)(2,1)}, bf16[128,640]{1,0:T(8,128)(2,1)}) custom-call(bf16[128,2048]{1,0:T(8,128)(2,1)} %bitcast.6, bf16[2048]{0:T(1024)(128)(2,1)} %again.1, bf16[64]{0:T(256)(128)(2,1)} %qgain.1, bf16[64]{0:T(256)(128)(2,1)} %kgain.1, bf16[2048]{0:T(1024)(128)(2,1)} %fgain.1, ...), custom_call_target="tpu_custom_call" | custom-call | tf_op jit(solution)/shard_map/block/pallas_call | solution.py:416
  67.8 1.8 %settle.1 = (bf16[32,2048]{1,0:T(8,128)(2,1)}, bf16[32,2048]{1,0:T(8,128)(2,1)}, bf16[32,640]{1,0:T(8,128)(2,1)}, bf16[128,640]{1,0:T(8,128)(2,1)}) custom-call(bf16[32,2048]{1,0:T(8,128)(2,1)} %get-tuple-element.12.refs_0_, bf16[32,2048]{1,0:T(8,128)(2,1)} %get-tuple-element.13.refs_1_, bf16[32,640]{1,0:T(8,128)(2,1)} %get-tuple-element.14.refs_2_, ...), custom_call_target="tpu_custom_call" | custom-call | tf_op jit(solution)/shard_map/settle/pallas_call | solution.py:456

commit v4 on v3

--- a/solution.py
+++ b/solution.py
@@ -119,6 +119,14 @@
             if far:
                 self.near(b)
             self.spread(b)
+
+        def hop(self, d):
+            b = sid(x, wrapz(z + d), c)
+            self.arrive(b)
+            self.near(b)
+
+        def out(self, d):
+            self.spread(sid(x, wrapz(z + d), c))
 
         def relay(self, d):
             b = sid(wrapx(x - ahead), wrapz(z + d), c)
@@ -183,6 +191,9 @@
             device_id_type=MESH,
         ).start()
     pltpu.make_async_copy(cpack.at[pl.ds(pl.multiple_of(x * PLANE, PLANE), PLANE)], xb.at[x], x_recv).start()
+    near, far = (1, -1, 2, -2), (5, -5)
+    rest = (4, -4, 6, -6, 3, -3, 7, -7)
+    rbq.start()
     def norm(i, carry):
         at = pl.ds(pl.multiple_of(i * 16, 16), 16)
         v = tok[at, :].astype(F32)
@@ -191,13 +202,13 @@
         return carry
 
     lax.fori_loop(0, 8, norm, 0)
-    near, far = (1, -1, 2, -2), (5, -5)
-    rest = (4, -4, 6, -6, 3, -3, 7, -7)
     for d in near:
         ra.here(d)
     ra.relay(0)
     for d in far:
         ra.here(d, True)
+    for d in far:
+        rbq.hop(d)
     pltpu.make_async_copy(xb, xb, x_recv).wait()
 
     def hand(k, carry):
@@ -214,7 +225,6 @@
 
     lax.fori_loop(1, PLANE, hand, 0)
     pltpu.make_async_copy(xb.at[:, low], eb.at[:, low], e_recv).start()
-    rbq.start()
     for d in near:
         ra.relay(d)
     ra.last(0)
@@ -228,7 +238,7 @@
     for d in near:
         rbq.here(d)
     for d in far:
-        rbq.here(d, True)
+        rbq.out(d)
     ra.relay(8)
     for d in rest:
         ra.relay(d)

time: 70.5 us -> 61.8 us (0.88)
  Pallas kernels: 69 us -> 61 us
    pallas_call x1, Pallas kernels: 67.2 us -> 59.1 us  [block(): pl.pallas_call(body, out_shape=(jax.ShapeDtypeStruct((32, 2048), BF), jax...]
where the time goes in v4:
time: 61.8 us; the launch traced here: 61.6 us
  Pallas kernels  61 us (99%)
  between operations  0.64 us (1%)
    pallas_call x1, Pallas kernels, block(): pl.pallas_call(body, out_shape=(jax.ShapeDtypeStruct((32, 2048), BF), jax...  59.1 us
    pallas_call x1, Pallas kernels, settle(): pl.pallas_call(settle_body, out_shape=[jax.ShapeDtypeStruct(v.shape, v.dt...  1.84 us

profile of v4, /device:TPU:1, one launch (start us, length us, event | category | flops | bytes accessed | tf_op | source)
XLA Modules:
  0.0 61.6 jit_solution(416226009281384768)
XLA Ops:
  0.6 59.1 %block.1 = (bf16[32,2048]{1,0:T(8,128)(2,1)}, bf16[32,2048]{1,0:T(8,128)(2,1)}, bf16[32,640]{1,0:T(8,128)(2,1)}, bf16[128,640]{1,0:T(8,128)(2,1)}) custom-call(bf16[128,2048]{1,0:T(8,128)(2,1)} %bitcast.6, bf16[2048]{0:T(1024)(128)(2,1)} %again.1, bf16[64]{0:T(256)(128)(2,1)} %qgain.1, bf16[64]{0:T(256)(128)(2,1)} %kgain.1, bf16[2048]{0:T(1024)(128)(2,1)} %fgain.1, ...), custom_call_target="tpu_custom_call" | custom-call | tf_op jit(solution)/shard_map/block/pallas_call | solution.py:426
  59.8 1.8 %settle.1 = (bf16[32,2048]{1,0:T(8,128)(2,1)}, bf16[32,2048]{1,0:T(8,128)(2,1)}, bf16[32,640]{1,0:T(8,128)(2,1)}, bf16[128,640]{1,0:T(8,128)(2,1)}) custom-call(bf16[32,2048]{1,0:T(8,128)(2,1)} %get-tuple-element.12.refs_0_, bf16[32,2048]{1,0:T(8,128)(2,1)} %get-tuple-element.13.refs_1_, bf16[32,640]{1,0:T(8,128)(2,1)} %get-tuple-element.14.refs_2_, ...), custom_call_target="tpu_custom_call" | custom-call | tf_op jit(solution)/shard_map/settle/pallas_call | solution.py:466

commit v5 on v4

--- a/solution.py
+++ b/solution.py
@@ -18,8 +18,9 @@
 
 
 def body(
-    tok, again, qgain, kgain, fgain, wq, wkv, wo, cache, prior, stretch,
+    tok_in, again_in, qgain_in, kgain_in, fgain_in, wq_in, wkv_in, wo_in, cache_in, prior_in, stretch_in,
     hidden, ffn, fresh, decode,
+    tok, again, qgain, kgain, fgain, wq, wkv, wo, cache, prior, stretch, i_sem,
     wa, wb, cpack, xb, eb, yb, normed, acc, qs, kvs, kvr, tb, rb, cosine, sine,
     a_send, a_recv, b_send, b_recv, x_send, x_recv, e_send, e_recv, y_send, y_recv, k_send, k_recv, t_send, t_recv,
 ):
@@ -54,6 +55,17 @@
     for k in range(1, NY):
         signal({"head": lax.rem(h + k, NY)})
 
+    taken = [
+        pltpu.make_async_copy(src, dst, i_sem.at[i])
+        for i, (src, dst) in enumerate(
+            ((wq_in, wq), (wkv_in, wkv), (wo_in, wo), (cache_in, cache), (prior_in, prior), (tok_in, tok),
+             (again_in, again), (qgain_in, qgain), (kgain_in, kgain), (fgain_in, fgain), (stretch_in, stretch))
+        )
+    ]
+    for copy in taken:
+        copy.start()
+    for copy in taken[:3]:
+        copy.wait()
     own = pl.ds(pl.multiple_of(s * 16, 16), 16)
     for head in range(NY):
 
@@ -108,7 +120,7 @@
                 self.push(b, toz(d))
 
         def start(self):
-            for d in (5, -5, 8):
+            for d in (5, -5):
                 self.push(s, toz(d))
             self.near(s)
             self.spread(s)
@@ -118,12 +130,16 @@
             self.arrive(b)
             if far:
                 self.near(b)
+                if d == 5:
+                    self.push(b, toz(-3))
             self.spread(b)
 
         def hop(self, d):
             b = sid(x, wrapz(z + d), c)
             self.arrive(b)
             self.near(b)
+            if d == 5:
+                self.push(b, toz(-3))
 
         def out(self, d):
             self.spread(sid(x, wrapz(z + d), c))
@@ -159,6 +175,8 @@
 
     ra, rbq = Ring(wa, a_send, a_recv), Ring(wb, b_send, b_recv)
     ra.start()
+    for copy in taken[3:]:
+        copy.wait()
     for head in range(NY):
 
         @pl.when(h == head)
@@ -377,9 +395,13 @@
 
     rbq.shared(x)
     project_out(x)
-    for d in far + (8,) + rest:
+    for d in far:
         rbq.last(d)
-    for d in (1, -1, 2):
+    rbq.shared(wrapx(x + 1))
+    project_out(wrapx(x + 1))
+    for d in (8,) + rest:
+        rbq.last(d)
+    for d in (-1, 2):
         rbq.shared(wrapx(x + d))
         project_out(wrapx(x + d))
 
@@ -419,7 +441,6 @@
 
 def block(*args):
     vmem = pl.BlockSpec(memory_space=pltpu.VMEM)
-    smem = pl.BlockSpec(memory_space=pltpu.SMEM)
     dma = pltpu.SemaphoreType.DMA
     many = pltpu.SemaphoreType.DMA((NX * PLANE,))
     cache_like = pltpu.VMEM((NX, PLANE, 4, 256), BF)
@@ -431,9 +452,21 @@
             jax.ShapeDtypeStruct((32, 640), BF),
             jax.ShapeDtypeStruct((128, 640), BF),
         ),
-        in_specs=[vmem] * 9 + [smem] * 2,
+        in_specs=[pl.BlockSpec(memory_space=pltpu.HBM)] * 11,
         out_specs=(vmem,) * 4,
         scratch_shapes=[
+            pltpu.VMEM((128, 2048), BF),
+            pltpu.VMEM((2048,), BF),
+            pltpu.VMEM((HD,), BF),
+            pltpu.VMEM((HD,), BF),
+            pltpu.VMEM((2048,), BF),
+            pltpu.VMEM((16, 320), BF),
+            pltpu.VMEM((16, 640), BF),
+            pltpu.VMEM((16, 320), BF),
+            pltpu.VMEM((128, 4, 640), BF),
+            pltpu.SMEM((128,), jnp.int32),
+            pltpu.SMEM((128,), jnp.int32),
+            pltpu.SemaphoreType.DMA((11,)),
             pltpu.VMEM((2048, A), BF),
             pltpu.VMEM((2048, B), BF),
             pltpu.VMEM((128, 4, 256), BF),

time: 61.8 us -> 60 us (0.971)
  Pallas kernels: 61 us -> 59.2 us
    pallas_call x1, Pallas kernels: 59.1 us -> 57.3 us  [block(): pl.pallas_call(body, out_shape=(jax.ShapeDtypeStruct((32, 2048), BF), jax...]
where the time goes in v5:
time: 60 us; the launch traced here: 59.8 us
  Pallas kernels  59.2 us (99%)
  between operations  0.64 us (1%)
    pallas_call x1, Pallas kernels, block(): pl.pallas_call(body, out_shape=(jax.ShapeDtypeStruct((32, 2048), BF), jax...  57.3 us
    pallas_call x1, Pallas kernels, settle(): pl.pallas_call(settle_body, out_shape=[jax.ShapeDtypeStruct(v.shape, v.dt...  1.84 us

profile of v5, /device:TPU:1, one launch (start us, length us, event | category | flops | bytes accessed | tf_op | source)
XLA Modules:
  0.0 59.8 jit_solution(932861103464614349)
XLA Ops:
  0.6 57.3 %block.1 = (bf16[32,2048]{1,0:T(8,128)(2,1)}, bf16[32,2048]{1,0:T(8,128)(2,1)}, bf16[32,640]{1,0:T(8,128)(2,1)}, bf16[128,640]{1,0:T(8,128)(2,1)}) custom-call(bf16[128,2048]{1,0:T(8,128)(2,1)} %bitcast.6, bf16[2048]{0:T(1024)(128)(2,1)} %again_in.1, bf16[64]{0:T(256)(128)(2,1)} %qgain_in.1, bf16[64]{0:T(256)(128)(2,1)} %kgain_in.1, ...), custom_call_target="tpu_custom_call" | custom-call | tf_op jit(solution)/shard_map/block/pallas_call | solution.py:447
  58.0 1.8 %settle.1 = (bf16[32,2048]{1,0:T(8,128)(2,1)}, bf16[32,2048]{1,0:T(8,128)(2,1)}, bf16[32,640]{1,0:T(8,128)(2,1)}, bf16[128,640]{1,0:T(8,128)(2,1)}) custom-call(bf16[32,2048]{1,0:T(8,128)(2,1)} %get-tuple-element.12.refs_0_, bf16[32,2048]{1,0:T(8,128)(2,1)} %get-tuple-element.13.refs_1_, bf16[32,640]{1,0:T(8,128)(2,1)} %get-tuple-element.14.refs_2_, ...), custom_call_target="tpu_custom_call" | custom-call | tf_op jit(solution)/shard_map/settle/pallas_call | solution.py:499

commit v6 on v5

--- a/solution.py
+++ b/solution.py
@@ -210,7 +210,7 @@
         ).start()
     pltpu.make_async_copy(cpack.at[pl.ds(pl.multiple_of(x * PLANE, PLANE), PLANE)], xb.at[x], x_recv).start()
     near, far = (1, -1, 2, -2), (5, -5)
-    rest = (4, -4, 6, -6, 3, -3, 7, -7)
+    rest = (3, 7, 4, 6, -7, -3, -6, -4, 8)
     rbq.start()
     def norm(i, carry):
         at = pl.ds(pl.multiple_of(i * 16, 16), 16)
@@ -227,6 +227,11 @@
         ra.here(d, True)
     for d in far:
         rbq.hop(d)
+    for d in near:
+        ra.relay(d)
+    ra.last(0)
+    for d in rest:
+        ra.here(d)
     pltpu.make_async_copy(xb, xb, x_recv).wait()
 
     def hand(k, carry):
@@ -243,12 +248,6 @@
 
     lax.fori_loop(1, PLANE, hand, 0)
     pltpu.make_async_copy(xb.at[:, low], eb.at[:, low], e_recv).start()
-    for d in near:
-        ra.relay(d)
-    ra.last(0)
-    ra.here(8)
-    for d in rest:
-        ra.here(d)
     for d in far:
         ra.relay(d)
     for d in near:
@@ -257,7 +256,6 @@
         rbq.here(d)
     for d in far:
         rbq.out(d)
-    ra.relay(8)
     for d in rest:
         ra.relay(d)
     for d in far:
@@ -274,10 +272,8 @@
             acc[...] += part
 
     project(x, True)
-    ra.last(8)
     for d in rest:
         ra.last(d)
-    rbq.here(8)
     for d in rest:
         rbq.here(d)
     ra.shared(wrapx(x + 1))
@@ -293,7 +289,6 @@
         rbq.last(d)
     ra.shared(wrapx(x + 2))
     project(wrapx(x + 2))
-    rbq.relay(8)
     for d in rest:
         rbq.relay(d)
 
@@ -399,7 +394,7 @@
         rbq.last(d)
     rbq.shared(wrapx(x + 1))
     project_out(wrapx(x + 1))
-    for d in (8,) + rest:
+    for d in rest:
         rbq.last(d)
     for d in (-1, 2):
         rbq.shared(wrapx(x + d))
@@ -490,17 +485,26 @@
 
 
 def settle_body(*refs):
-    for src, dst in zip(refs[:4], refs[4:]):
-        dst[...] = src[...]
+    made, out, held, into, onto = refs[:4], refs[4:8], refs[8:12], refs[12], refs[13]
+    first = [pltpu.make_async_copy(made[i], held[i], into.at[i]) for i in range(4)]
+    then = [pltpu.make_async_copy(held[i], out[i], onto.at[i]) for i in range(4)]
+    for copy in first:
+        copy.start()
+    for i in range(4):
+        first[i].wait()
+        then[i].start()
+    for copy in then:
+        copy.wait()
 
 
 def settle(*made):
-    vmem = pl.BlockSpec(memory_space=pltpu.VMEM)
+    hbm = pl.BlockSpec(memory_space=pltpu.HBM)
     return pl.pallas_call(
         settle_body,
         out_shape=[jax.ShapeDtypeStruct(v.shape, v.dtype) for v in made],
-        in_specs=[vmem] * 4,
-        out_specs=[vmem] * 4,
+        in_specs=[hbm] * 4,
+        out_specs=[hbm] * 4,
+        scratch_shapes=[pltpu.VMEM(v.shape, v.dtype) for v in made] + [pltpu.SemaphoreType.DMA((4,))] * 2,
         name="settle",
     )(*made)
 

time: 60 us -> 59 us (0.983)
  Pallas kernels: 59.2 us -> 57.8 us
    pallas_call x1, Pallas kernels: 57.3 us -> 56 us  [block(): pl.pallas_call(body, out_shape=(jax.ShapeDtypeStruct((32, 2048), BF), jax...]
where the time goes in v6:
time: 59 us; the launch traced here: 58.4 us
  Pallas kernels  57.8 us (98%)
  between operations  0.64 us (1%)
    pallas_call x1, Pallas kernels, block(): pl.pallas_call(body, out_shape=(jax.ShapeDtypeStruct((32, 2048), BF), jax...  56 us
    pallas_call x1, Pallas kernels, settle(): pl.pallas_call(settle_body, out_shape=[jax.ShapeDtypeStruct(v.shape, v.dt...  1.8 us

profile of v6, /device:TPU:1, one launch (start us, length us, event | category | flops | bytes accessed | tf_op | source)
XLA Modules:
  0.0 58.4 jit_solution(7216442565290286461)
XLA Ops:
  0.6 56.0 %block.1 = (bf16[32,2048]{1,0:T(8,128)(2,1)}, bf16[32,2048]{1,0:T(8,128)(2,1)}, bf16[32,640]{1,0:T(8,128)(2,1)}, bf16[128,640]{1,0:T(8,128)(2,1)}) custom-call(bf16[128,2048]{1,0:T(8,128)(2,1)} %bitcast.6, bf16[2048]{0:T(1024)(128)(2,1)} %again_in.1, bf16[64]{0:T(256)(128)(2,1)} %qgain_in.1, bf16[64]{0:T(256)(128)(2,1)} %kgain_in.1, ...), custom_call_target="tpu_custom_call" | custom-call | tf_op jit(solution)/shard_map/block/pallas_call | solution.py:442
  56.6 1.8 %settle.1 = (bf16[32,2048]{1,0:T(8,128)(2,1)}, bf16[32,2048]{1,0:T(8,128)(2,1)}, bf16[32,640]{1,0:T(8,128)(2,1)}, bf16[128,640]{1,0:T(8,128)(2,1)}) custom-call(bf16[32,2048]{1,0:T(8,128)(2,1)} %get-tuple-element.12.refs_0_, bf16[32,2048]{1,0:T(8,128)(2,1)} %get-tuple-element.13.refs_1_, bf16[32,640]{1,0:T(8,128)(2,1)} %get-tuple-element.14.refs_2_, ...), custom_call_target="tpu_custom_call" | custom-call | tf_op jit(solution)/shard_map/settle/pallas_call | solution.py:502
